TPU v7x, 32 devices: a whole 2x2x4 slice. The times are simulated.
32 devices in a mesh: chan: 4 (over y, x), tm: 8 (over z, core).
Axes of the slice: x: 2, y: 2, z: 4, core: 2. Of those that a mesh axis runs over, the one named last changes fastest.
Arguments:
- samples: bfloat16 [16, 2048, 1024], P('tm', 'chan'), may hold values from -6 to 6
- valid: int32 [16, 4], P('tm'), may hold values from 0 to 1, as said below
- plan: int32 [3, 4], replicated, may hold values from 0 to 3, as said below
Outputs:
- correlations: float32 [2048, 3, 129], P(('chan', 'tm'))
Inputs may be any that keep to these rules, and one draw needn't show every extreme that they name: In each round every block is paired with another block and that block with it: plan[r, plan[r, b]] = b and plan[r, b] != b; no block meets the same partner in two rounds. valid[15, b] = 1 for every block b.
All inputs are finite; a program needn't handle non-finite values.
Results may differ from a plain program's by a relative error of at most 0.0053.
Values may be sent and summed in bfloat16 or wider, within the bound.
No kernel may reach another device: no remote copies, remote signals or barrier semaphores. Data moves between devices by JAX's collectives and lax.ppermute only.
A program may use at most 64 MiB of HBM per device.

v0:
```python
import functools
import math

import jax
import jax.numpy as jnp
import numpy as np
from jax import lax
from jax.experimental import pallas as pl
from jax.experimental.pallas import tpu as pltpu
from jax.sharding import PartitionSpec as P


LAGS = 129
LANES = 128
STEP = 16
PARTS = 2


def dft_table(length, count):
    sample_idx = np.arange(length, dtype=np.int64)[:, None]
    bin_idx = np.arange(count, dtype=np.int64)[None, :]
    phase = (sample_idx * bin_idx % length).astype(np.float64) * (2.0 * math.pi / length)
    return np.concatenate([np.cos(phase), -np.sin(phase)], axis=1)


def lag_table(count, length, shifts, sign):
    bin_idx = np.arange(count, dtype=np.int64)[:, None]
    phase = (bin_idx * shifts[None, :] % length).astype(np.float64) * (2.0 * math.pi / length)
    return np.concatenate([0.25 * np.cos(phase), -0.25 * sign * np.sin(phase)], axis=0)


def high_low(table):
    high = jnp.asarray(table.astype(np.float32)).astype(jnp.bfloat16)
    low = (jnp.asarray(table.astype(np.float32)) - high.astype(jnp.float32)).astype(jnp.bfloat16)
    return high, low


def split(value):
    high = value.astype(jnp.bfloat16)
    return high, (value - high.astype(jnp.float32)).astype(jnp.bfloat16)


def whiten(pieces, masks, table, spec, white):
    windows, rows, length = pieces[0][2].shape
    bins = length // 2
    data = jnp.concatenate([piece[...].reshape(windows * rows, length) for _, _, piece in pieces], axis=0)
    spec[: data.shape[0], :] = jnp.dot(data, table[...], preferred_element_type=jnp.float32)
    for order, (half, slot, _) in enumerate(pieces):
        for window in range(windows):
            present = masks[half][window, lax.axis_index("chan") ^ slot].astype(jnp.float32)
            start = (order * windows + window) * rows

            def body(step, carry):
                row = pl.multiple_of(step * STEP, STEP)
                real = spec[pl.ds(start + row, STEP), :bins]
                imag = spec[pl.ds(start + row, STEP), bins:]
                power = real * real + imag * imag
                level = jnp.mean(power, axis=1, keepdims=True)
                scale = lax.rsqrt(power + 0.1 * level + 1e-06) * present
                target = white(half, slot)
                target[window, pl.ds(row, STEP), :bins] = (real * scale).astype(jnp.bfloat16)
                target[window, pl.ds(row, STEP), bins:] = (imag * scale).astype(jnp.bfloat16)
                return carry

            lax.fori_loop(0, rows // STEP, body, 0, unroll=True)


def cross(white, first, second, row, rows):
    bins = white.shape[3] // 2
    real_sum, imag_sum = None, None
    for window in range(white.shape[1]):
        own = white[first, window, pl.ds(row, rows), :].astype(jnp.float32)
        other = white[second, window, pl.ds(row, rows), :].astype(jnp.float32)
        own_re, own_im, other_re, other_im = own[:, :bins], own[:, bins:], other[:, :bins], other[:, bins:]
        real_part = own_re * other_re + own_im * other_im
        imag_part = own_im * other_re - own_re * other_im
        real_sum = real_part if real_sum is None else real_sum + real_part
        imag_sum = imag_part if imag_sum is None else imag_sum + imag_part
    return real_sum, imag_sum


def list_pairs(plan, lead, mate):
    rounds, blocks = plan.shape
    place = 0
    for step in range(rounds):
        place = step * (blocks // 2)
        for block in range(blocks):
            partner = plan[step, block]
            lead[place] = block
            mate[place] = partner
            place = place + (partner > block).astype(jnp.int32)


def early_kernel(slots, valid, other, *refs):
    pieces, (table, out, spec) = refs[:-3], refs[-3:]
    place = {key: order for order, key in enumerate(slots)}
    listed = [(half, slot, piece) for (half, slot), piece in zip(slots, pieces, strict=True)]
    whiten(listed, (valid, other), table, spec, lambda half, slot: out.at[place[half, slot]])


def gather_white(half, slots, late, early, white):
    for order, (early_half, slot) in enumerate(slots):
        if early_half == half:
            white[slot] = early[order]
    return [(half, slot, piece) for slot, piece in late]


def first_kernel(slots, late, plan, valid, other, *refs):
    pieces, (early, table, stack, spec, white, lead, mate) = refs[:-7], refs[-7:]
    here = lax.axis_index("chan")
    list_pairs(plan, lead, mate)
    listed = gather_white(0, slots, list(zip(late, pieces, strict=True)), early, white)
    whiten(listed, (valid, other), table, spec, lambda half, slot: white.at[slot])
    pairs, rows, width = stack.shape
    bins = width // 2
    for pair in range(pairs):
        first, second = lead[pair] ^ here, mate[pair] ^ here

        def body(step, carry):
            row = pl.multiple_of(step * STEP, STEP)
            real_sum, imag_sum = cross(white, first, second, row, STEP)
            stack[pair, pl.ds(row, STEP), :bins] = real_sum
            stack[pair, pl.ds(row, STEP), bins:] = imag_sum
            return carry

        lax.fori_loop(0, rows // STEP, body, 0, unroll=True)


def second_kernel(rounds, slots, late, part, plan, valid, other, *refs):
    head, refs = refs[: len(late)], refs[len(late) :]
    done, refs = refs[:part], refs[part:]
    early, table, stack, lag_hi, lag_lo, end_hi, end_lo, out, spec, white, hi, lo, main, extra, lead, mate = refs
    here = lax.axis_index("chan")
    list_pairs(plan, lead, mate)
    rows = head[0].shape[1]
    base = part * rows
    for order, (half, slot) in enumerate(slots):
        if half == 1:
            white[slot] = early[order, :, base : base + rows, :]
    whiten([(1, slot, piece) for slot, piece in zip(late, head, strict=True)], (valid, other), table, spec, lambda half, slot: white.at[slot])
    pairs, _, width = stack.shape
    bins = width // 2
    for pair in range(pairs):
        first, second = lead[pair] ^ here, mate[pair] ^ here

        def body(step, carry):
            row = pl.multiple_of(step * STEP, STEP)
            real_sum, imag_sum = cross(white, first, second, row, STEP)
            real_sum = real_sum + stack[pair, pl.ds(base + row, STEP), :bins]
            imag_sum = imag_sum + stack[pair, pl.ds(base + row, STEP), bins:]
            place = pl.ds(pl.multiple_of(pair * rows + row, STEP), STEP)
            hi[place, :bins], lo[place, :bins] = split(real_sum)
            hi[place, bins:], lo[place, bins:] = split(imag_sum)
            return carry

        lax.fori_loop(0, rows // STEP, body, 0, unroll=True)
    dot = functools.partial(jnp.dot, preferred_element_type=jnp.float32)
    main[...] = dot(hi[...], lag_hi[...]) + dot(lo[...], lag_hi[...]) + dot(hi[...], lag_lo[...])
    across = functools.partial(
        lax.dot_general, dimension_numbers=(((1,), (1,)), ((), ())), preferred_element_type=jnp.float32
    )
    ends = across(end_hi[...], hi[...]) + across(end_hi[...], lo[...]) + across(end_lo[...], hi[...])
    extra[...] = jnp.zeros_like(extra)
    group = (out.shape[2] - 8) // rounds
    zones = rows // group
    for earlier, ref in enumerate(done):
        out[:, earlier * zones : (earlier + 1) * zones] = ref[:, earlier * zones : (earlier + 1) * zones]
    first_zone = part * zones
    per_round = pairs // rounds
    for pair in range(pairs):
        step = pair // per_round
        count = 0
        for mask in (valid, other):
            for window in range(mask.shape[0]):
                count = count + mask[window, lead[pair]] * mask[window, mate[pair]]
        count = jnp.full((1, LANES), count.astype(jnp.float32))
        for side in range(2):
            block = (lead, mate)[side][pair]
            extra[block, rounds + step : rounds + step + 1, :] = count
            value = main[pair * rows : (pair + 1) * rows, side * LANES : (side + 1) * LANES]
            value = value.astype(jnp.bfloat16).reshape(zones, group, LANES)
            out[block, first_zone : first_zone + zones, step * group : (step + 1) * group, :] = value
            extra[block, step : step + 1, :rows] = ends[side : side + 1, pair * rows : (pair + 1) * rows]
    for block in range(out.shape[0]):
        tail = extra[block].astype(jnp.bfloat16)
        for zone in range(zones):
            out[block, first_zone + zone, rounds * group : rounds * group + 8, :] = tail


def cut_kernel(keys, zone_ranges, samples, *refs):
    outs, sems = refs[: len(keys)], refs[len(keys)]
    here, half = lax.axis_index("chan"), lax.axis_index("tm") % 2
    copies = []
    for order, ((half_step, chan_step), (start, count)) in enumerate(zip(keys, zone_ranges, strict=True)):
        source = samples.at[:, start : start + count, half ^ half_step, here ^ chan_step]
        copy = pltpu.make_async_copy(source, outs[order], sems.at[order])
        copy.start()
        copies.append(copy)
    for copy in copies:
        copy.wait()


def last_kernel(rounds, per_part, parts, out):
    blocks, zones, _, _ = parts.shape
    group = out.shape[1] // blocks
    lane = lax.broadcasted_iota(jnp.int32, (group, LANES), 1)
    row = lax.broadcasted_iota(jnp.int32, (group, LANES), 0)
    chosen = lane == row + lax.axis_index("tm") // 2 % per_part * group
    inverse = None
    for block in range(blocks):
        total = parts[block, 0].astype(jnp.float32)
        for zone in range(1, zones):
            total = total + parts[block, zone].astype(jnp.float32)
        tail = total[rounds * group : rounds * group + 8]
        if inverse is None:
            inverse = 1.0 / tail[rounds : 2 * rounds]
        for step in range(rounds):
            scale = inverse[step : step + 1]
            rows = slice(block * group, (block + 1) * group)
            out[step, rows, :LANES] = total[step * group : (step + 1) * group] * scale
            end = jnp.where(chosen, tail[step : step + 1] * scale, 0.0)
            out[step, rows, LANES:] = jnp.sum(end, axis=1, keepdims=True)


def by_channels(samples, valid, plan):
    chan_count, time_count = lax.axis_size("chan"), lax.axis_size("tm")
    windows, block_width, length = samples.shape
    bins = length // 2
    rounds = plan.shape[0]
    maxlag = (LAGS - 1) // 2
    zones = time_count // 2
    group = block_width // (time_count * chan_count)
    rows = zones * group

    smem = pl.BlockSpec(memory_space=pltpu.SMEM)
    vmem = pl.BlockSpec(memory_space=pltpu.VMEM)
    params = pltpu.CompilerParams(vmem_limit_bytes=12 * 1024 * 1024)
    grouped = samples.reshape(windows, zones, 2, chan_count, group, length)

    def cut(keys, zone_ranges):
        pieces = pl.pallas_call(
            functools.partial(cut_kernel, keys, zone_ranges),
            out_shape=[
                jax.ShapeDtypeStruct((windows, count, group, length), samples.dtype) for _, count in zone_ranges
            ],
            in_specs=[pl.BlockSpec(memory_space=pltpu.HBM)],
            out_specs=[vmem] * len(keys),
            scratch_shapes=[pltpu.SemaphoreType.DMA((len(keys),))],
            compiler_params=pltpu.CompilerParams(vmem_limit_bytes=8 * 1024 * 1024),
        )(pltpu.with_memory_space_constraint(grouped, pltpu.HBM))
        return [piece.reshape(windows, count * group, length) for piece, (_, count) in zip(pieces, zone_ranges, strict=True)]

    def partners(half_step, chan_step):
        return [
            (a * time_count + t, (a ^ chan_step) * time_count + (t ^ half_step))
            for a in range(chan_count)
            for t in range(time_count)
        ]

    def is_late(chan_step):
        return chan_step & (chan_step - 1) == 0 and chan_step > 0

    early_steps = [s for s in range(chan_count - 1, -1, -1) if not is_late(s)]
    late_steps = [s for s in range(chan_count) if is_late(s)]
    early_slots = [(h, s) for s in early_steps for h in range(2)]
    late_first = [(0, s) for s in late_steps]
    late_second = [(1, s) for s in late_steps]
    per_part = zones // PARTS
    keys = early_slots + late_first + late_second * PARTS
    ranges = [(0, zones)] * (len(early_slots) + len(late_first))
    ranges += [(part * per_part, per_part) for part in range(PARTS) for _ in late_second]
    pieces = cut(keys[:1], ranges[:1])
    pieces += cut(keys[1:], ranges[1:])
    received, sent_pieces = [], 0
    for key, piece in zip(keys, pieces, strict=True):
        if key != (0, 0):
            piece = lax.ppermute(piece, ("chan", "tm"), partners(*key))
            sent_pieces += 1
        received.append(piece)
    early_pieces, received = received[: len(early_slots)], received[len(early_slots) :]
    first_pieces, second_pieces = received[: len(late_steps)], received[len(late_steps) :]

    other = lax.ppermute(valid, ("chan", "tm"), partners(1, 0))
    pairs = rounds * (chan_count // 2)
    table = jnp.asarray(dft_table(length, bins).astype(np.float32)).astype(jnp.bfloat16)
    shifts = np.arange(-maxlag, maxlag, dtype=np.int64)
    lags = np.concatenate([lag_table(bins, length, shifts, s) for s in (1.0, -1.0)], axis=1)
    lag_hi, lag_lo = high_low(lags)
    last = np.array([maxlag], dtype=np.int64)
    ends = np.concatenate([lag_table(bins, length, last, s) for s in (1.0, -1.0)], axis=1).T
    end_hi, end_lo = high_low(np.pad(ends, ((0, 14), (0, 0))))

    lists = [pltpu.SMEM((pairs + 1,), jnp.int32)] * 2

    def spec_scratch(pieces, height):
        return pltpu.VMEM((pieces * windows * height, length), jnp.float32)

    def white_scratch(height):
        return pltpu.VMEM((chan_count, windows, height, length), jnp.bfloat16)

    early = pl.pallas_call(
        functools.partial(early_kernel, early_slots),
        out_shape=jax.ShapeDtypeStruct((len(early_slots), windows, rows, length), jnp.bfloat16),
        in_specs=[smem] * 2 + [vmem] * (len(early_slots) + 1),
        out_specs=vmem,
        scratch_shapes=[spec_scratch(len(early_slots), rows)],
        compiler_params=params,
        name="early",
    )(valid, other, *early_pieces, table)
    stack = pl.pallas_call(
        functools.partial(first_kernel, early_slots, late_steps),
        out_shape=jax.ShapeDtypeStruct((pairs, rows, length), jnp.float32),
        in_specs=[smem] * 3 + [vmem] * (len(late_steps) + 2),
        out_specs=vmem,
        scratch_shapes=[spec_scratch(len(late_steps), rows), white_scratch(rows), *lists],
        compiler_params=params,
        name="first_half",
    )(plan, valid, other, *first_pieces, early, table)
    height = rounds * group + 8
    part_rows = per_part * group
    sent = []
    for part in range(PARTS):
        heads = second_pieces[part * len(late_steps) : (part + 1) * len(late_steps)]
        sent.append(
            pl.pallas_call(
                functools.partial(second_kernel, rounds, early_slots, late_steps, part),
                out_shape=jax.ShapeDtypeStruct((chan_count, zones, height, LANES), jnp.bfloat16),
                in_specs=[smem] * 3 + [vmem] * (len(late_steps) + part + 7),
                out_specs=vmem,
                scratch_shapes=[
                    spec_scratch(len(late_steps), part_rows),
                    white_scratch(part_rows),
                    pltpu.VMEM((pairs * part_rows, length), jnp.bfloat16),
                    pltpu.VMEM((pairs * part_rows, length), jnp.bfloat16),
                    pltpu.VMEM((pairs * part_rows, 2 * LANES), jnp.float32),
                    pltpu.VMEM((chan_count, 8, LANES), jnp.float32),
                    *lists,
                ],
                compiler_params=params,
            )(plan, valid, other, *heads, *sent, early, table, stack, lag_hi, lag_lo, end_hi, end_lo)
        )
    sent = sent[-1]
    same_half = [[a * time_count + z * 2 + c for a in range(chan_count) for z in range(zones)] for c in range(2)]
    parts = lax.all_to_all(
        sent.reshape(chan_count * zones, height, LANES),
        ("chan", "tm"),
        split_axis=0,
        concat_axis=0,
        tiled=True,
        axis_index_groups=same_half,
    ).reshape(chan_count, zones, height, LANES)
    result = pl.pallas_call(
        functools.partial(last_kernel, rounds, per_part),
        out_shape=jax.ShapeDtypeStruct((rounds, chan_count * group, LAGS), jnp.float32),
        in_specs=[vmem],
        out_specs=vmem,
        compiler_params=params,
        name="finish",
    )(parts)
    return result.transpose(1, 0, 2)


def table_on_device(length, count):
    sample_idx = jnp.arange(length, dtype=jnp.int32)[:, None]
    bin_idx = jnp.arange(count, dtype=jnp.int32)[None, :]
    phase = (sample_idx * bin_idx % length).astype(jnp.float32) * (2.0 * math.pi / length)
    return jnp.concatenate([jnp.cos(phase), -jnp.sin(phase)], axis=1).astype(jnp.bfloat16)


def lags_on_device(first_bin, count, length, maxlag):
    bin_idx = (first_bin + jnp.arange(count, dtype=jnp.int32))[:, None]
    shifts = jnp.arange(-maxlag, maxlag + 1, dtype=jnp.int32)[None, :]
    phase = (bin_idx * shifts % length).astype(jnp.float32) * (2.0 * math.pi / length)
    return jnp.concatenate([0.25 * jnp.cos(phase), -0.25 * jnp.sin(phase)], axis=0)


def by_bins(samples, valid, plan):
    chan_count = lax.axis_size("chan")
    windows_here, block_width, length = samples.shape
    bin_count = length // 2
    share = bin_count // chan_count
    all_channels = block_width * chan_count
    rounds = plan.shape[0]
    maxlag = (LAGS - 1) // 2
    table = table_on_device(length, bin_count)
    table = (
        table.reshape(length, 2, chan_count, share)
        .transpose(0, 2, 1, 3)
        .reshape(length, 2 * bin_count)
    )
    spec = jnp.dot(samples.reshape(-1, length), table, preferred_element_type=jnp.float32)
    spec = spec.reshape(windows_here, block_width, chan_count, 2, share)
    power = spec[:, :, :, 0] * spec[:, :, :, 0] + spec[:, :, :, 1] * spec[:, :, :, 1]
    level = jnp.mean(power, axis=(2, 3), keepdims=True)
    white = spec / jnp.sqrt(power + 0.1 * level + 1e-06)[:, :, :, None, :]
    white = white.astype(jnp.bfloat16).reshape(windows_here, block_width, 2 * bin_count)
    moved = lax.all_to_all(white, "chan", split_axis=2, concat_axis=1, tiled=True)
    blocks = moved.reshape(windows_here, chan_count, block_width, 2, share)
    mask = valid.astype(jnp.float32)
    weights = jnp.stack([mask * jnp.take(mask, plan[step], axis=1) for step in range(rounds)])
    totals = lax.psum(jnp.sum(weights, axis=1), "tm")
    own = blocks.astype(jnp.float32)
    partial_list = []
    for step in range(rounds):
        other = jnp.take(blocks, plan[step], axis=1).astype(jnp.float32)
        real_part = own[:, :, :, 0] * other[:, :, :, 0] + own[:, :, :, 1] * other[:, :, :, 1]
        imag_part = own[:, :, :, 1] * other[:, :, :, 0] - own[:, :, :, 0] * other[:, :, :, 1]
        product = jnp.stack([real_part, imag_part], axis=3)
        summed = jnp.einsum("wb,wbicf->bicf", weights[step], product)
        summed = summed / totals[step][:, None, None, None]
        partial_list.append(summed.reshape(all_channels, 2 * share))
    partial_value = jnp.stack(partial_list, axis=1)
    lags = lags_on_device(lax.axis_index("chan") * share, share, length, maxlag)
    return lax.psum_scatter(
        jnp.einsum("crk,kl->crl", partial_value, lags, precision=lax.Precision.HIGHEST),
        ("chan", "tm"),
        scatter_dimension=0,
        tiled=True,
    )


def shards(samples, valid, plan):
    chan_count, time_count = lax.axis_size("chan"), lax.axis_size("tm")
    block_width = samples.shape[1]
    rows_each = block_width // (time_count * chan_count)
    whole_tiles = rows_each > 0 and rows_each % STEP == 0 and block_width == rows_each * time_count * chan_count
    whole_tiles = whole_tiles and time_count % (2 * PARTS) == 0
    powers = chan_count & (chan_count - 1) == 0 and chan_count > 1 and time_count % 2 == 0
    if whole_tiles and powers and rows_each * time_count // 2 <= LANES and 2 * plan.shape[0] <= 8:
        return by_channels(samples, valid, plan)
    return by_bins(samples, valid, plan)


def solution(mesh):
    return jax.shard_map(
        shards,
        mesh=mesh,
        in_specs=(P("tm", "chan", None), P("tm", None), P()),
        out_specs=P(("chan", "tm"), None, None),
        check_vma=False,
    )
```

profile of v0, /device:TPU:0, one launch (start us, length us, event | category | flops | bytes accessed | tf_op | source)
XLA Modules:
  0.0 50.3 jit_solution(13456940509782625204)
XLA Ops:
  0.0 1.1 %shard_map.83 = bf16[2,4,16,1024]{3,2,1,0:T(8,128)(2,1)S(1)} custom-call(bf16[2,4,2,4,16,1024]{5,4,3,2,1,0:T(8,128)(2,1)} %bitcast.26), custom_call_target="tpu_custom_call" | custom-call | tf_op jit(solution)/shard_map/pallas_call | solution.py:241
  1.1 4.0 %collective-permute-start.5 = (bf16[2,64,1024]{2,1,0:T(8,128)(2,1)S(1)}, bf16[2,64,1024]{2,1,0:T(8,128)(2,1)S(1)}, u32[]{:S(2)}, u32[]{:S(2)}) collective-permute-start(bf16[2,64,1024]{2,1,0:T(8,128)(2,1)S(1)} %bitcast.16), channel_id=1, source_target_pairs={{0,24},{1,25},{2,26},{3,27},{4,28},{5,29},{6,30},{7,31},{8,16},{9,... | collective-permute-start | bytes 786440 | tf_op jit(solution)/shard_map/ppermute | solution.py:277
  5.1 1.5 %shard_map.82 = (bf16[2,4,16,1024]{3,2,1,0:T(8,128)(2,1)S(1)}, bf16[2,4,16,1024]{3,2,1,0:T(8,128)(2,1)S(1)}, bf16[2,4,16,1024]{3,2,1,0:T(8,128)(2,1)S(1)}, bf16[...) custom-call(bf16[2,4,2,4,16,1024]{5,4,3,2,1,0:T(8,128)(2,1)} %bitcast.27), custom_call_target="tpu_custom_call" | custom-call | tf_op jit(solution)/shard_map/pallas_call | solution.py:241
  6.6 0.1 collective-permute-start.6
  6.7 0.1 collective-permute-start.7
  6.8 1.9 %collective-permute-start.8 = (bf16[2,64,1024]{2,1,0:T(8,128)(2,1)S(1)}, bf16[2,64,1024]{2,1,0:T(8,128)(2,1)S(1)}, u32[]{:S(2)}, u32[]{:S(2)}) collective-permute-start(bf16[2,64,1024]{2,1,0:T(8,128)(2,1)S(1)} %bitcast.19), channel_id=1, source_target_pairs={{0,8},{1,9},{2,10},{3,11},{4,12},{5,13},{6,14},{7,15},{8,0},{9,1},... | collective-permute-start | bytes 786440 | tf_op jit(solution)/shard_map/ppermute | solution.py:277
  8.8 0.0 collective-permute-start
  8.8 1.2 %collective-permute-done.other = s32[2,4]{1,0:T(2,128)S(1)} collective-permute-done((s32[2,4]{1,0:T(2,128)S(1)}, s32[2,4]{1,0:T(2,128)S(1)}, u32[]{:S(2)}, u32[]{:S(2)}) %collective-permute-start) | collective-permute-done | bytes 64 | tf_op jit(solution)/shard_map/ppermute | solution.py:283
  9.9 1.5 %collective-permute-start.9 = (bf16[2,64,1024]{2,1,0:T(8,128)(2,1)S(1)}, bf16[2,64,1024]{2,1,0:T(8,128)(2,1)S(1)}, u32[]{:S(2)}, u32[]{:S(2)}) collective-permute-start(bf16[2,64,1024]{2,1,0:T(8,128)(2,1)S(1)} %bitcast.18), channel_id=1, source_target_pairs={{0,16},{1,17},{2,18},{3,19},{4,20},{5,21},{6,22},{7,23},{8,24},{9,... | collective-permute-start | bytes 786440 | tf_op jit(solution)/shard_map/ppermute | solution.py:277
  11.4 0.8 %collective-permute-done.5.refs_0_ = bf16[2,64,1024]{2,1,0:T(8,128)(2,1)S(1)} collective-permute-done((bf16[2,64,1024]{2,1,0:T(8,128)(2,1)S(1)}, bf16[2,64,1024]{2,1,0:T(8,128)(2,1)S(1)}, u32[]{:S(2)}, u32[]{:S(2)}) %collective-permute-start.5) | collective-permute-done | bytes 262176 | tf_op jit(solution)/shard_map/ppermute | solution.py:277
  12.3 0.0 collective-permute-start.3
  12.3 5.2 %collective-permute-done.6.refs_1_ = bf16[2,64,1024]{2,1,0:T(8,128)(2,1)S(1)} collective-permute-done((bf16[2,64,1024]{2,1,0:T(8,128)(2,1)S(1)}, bf16[2,64,1024]{2,1,0:T(8,128)(2,1)S(1)}, u32[]{:S(2)}, u32[]{:S(2)}) %collective-permute-start.6) | collective-permute-done | bytes 262176 | tf_op jit(solution)/shard_map/ppermute | solution.py:277
  17.5 1.9 %collective-permute-start.4 = (bf16[2,32,1024]{2,1,0:T(8,128)(2,1)S(1)}, bf16[2,32,1024]{2,1,0:T(8,128)(2,1)S(1)}, u32[]{:S(2)}, u32[]{:S(2)}) collective-permute-start(bf16[2,32,1024]{2,1,0:T(8,128)(2,1)S(1)} %bitcast.24), channel_id=1, source_target_pairs={{0,17},{1,16},{2,19},{3,18},{4,21},{5,20},{6,23},{7,22},{8,25},{9,... | collective-permute-start | bytes 393224 | tf_op jit(solution)/shard_map/ppermute | solution.py:277
  19.3 0.0 collective-permute-done.7.refs_3_
  19.3 0.0 collective-permute-start.2
  19.4 4.7 %collective-permute-done.8.refs_0_ = bf16[2,64,1024]{2,1,0:T(8,128)(2,1)S(1)} collective-permute-done((bf16[2,64,1024]{2,1,0:T(8,128)(2,1)S(1)}, bf16[2,64,1024]{2,1,0:T(8,128)(2,1)S(1)}, u32[]{:S(2)}, u32[]{:S(2)}) %collective-permute-start.8) | collective-permute-done | bytes 262176 | tf_op jit(solution)/shard_map/ppermute | solution.py:277
  24.1 0.0 collective-permute-start.1
  24.1 2.1 %early.1.refs_2_.refs_3_ = bf16[4,2,64,1024]{3,2,1,0:T(8,128)(2,1)S(1)} custom-call(s32[2,4]{1,0:T(2,128)S(1)} %copy-done.6, s32[2,4]{1,0:T(2,128)S(1)} %collective-permute-done.other, bf16[2,64,1024]{2,1,0:T(8,128)(2,1)S(1)} %collective-permute-done.5.refs_0_, bf16[2,64,1024]{2,1,0:T(8,128)(2,1)S(1)} %collective-permute-done.6.refs_1_, ...), custom_call_target="tpu_custom_call" | custom-call | tf_op jit(solution)/shard_map/early/pallas_call | solution.py:301
  26.2 0.0 copy-start.1
  26.2 0.0 copy-start.2
  26.2 0.0 copy-start.3
  26.2 0.0 copy-start.4
  26.2 0.0 collective-permute-done.9.refs_1_
  26.3 2.1 %first_half.1.refs_4_.refs_5_ = f32[6,64,1024]{2,1,0:T(8,128)S(1)} custom-call(s32[3,4]{1,0:T(4,128)S(1)} %copy-done.5, s32[2,4]{1,0:T(2,128)S(1)} %copy-done.6, s32[2,4]{1,0:T(2,128)S(1)} %collective-permute-done.other, bf16[2,64,1024]{2,1,0:T(8,128)(2,1)S(1)} %collective-permute-done.8.refs_0_, bf16[2,64,1024]{2,1,0:T(8,128)(2,1)S(1)} %collective-permute-done.9.refs_1_, ...), custom_call_target="tpu_custom_call" | custom-call | tf_op jit(solution)/shard_map/first_half/pallas_call | solution.py:310
  28.4 0.0 collective-permute-done.3.refs_0_
  28.4 0.0 collective-permute-done.4.refs_1_
  28.4 2.3 %shard_map.84.refs_2_ = bf16[4,4,56,128]{3,2,1,0:T(8,128)(2,1)S(1)} custom-call(s32[3,4]{1,0:T(4,128)S(1)} %copy-done.5, s32[2,4]{1,0:T(2,128)S(1)} %copy-done.6, s32[2,4]{1,0:T(2,128)S(1)} %collective-permute-done.other, bf16[2,32,1024]{2,1,0:T(8,128)(2,1)S(1)} %collective-permute-done.3.refs_0_, bf16[2,32,1024]{2,1,0:T(8,128)(2,1)S(1)} %collective-permute-done.4.refs_1_, ...), custom_call_target="tpu_custom_call" | custom-call | tf_op jit(solution)/shard_map/pallas_call | solution.py:325
  30.7 0.0 collective-permute-done.2.refs_1_
  30.8 0.0 collective-permute-done.1.refs_0_
  30.8 2.3 %shard_map.85 = bf16[4,4,56,128]{3,2,1,0:T(8,128)(2,1)S(1)} custom-call(s32[3,4]{1,0:T(4,128)S(1)} %copy-done.5, s32[2,4]{1,0:T(2,128)S(1)} %copy-done.6, s32[2,4]{1,0:T(2,128)S(1)} %collective-permute-done.other, bf16[2,32,1024]{2,1,0:T(8,128)(2,1)S(1)} %collective-permute-done.1.refs_0_, bf16[2,32,1024]{2,1,0:T(8,128)(2,1)S(1)} %collective-permute-done.2.refs_1_, ...), custom_call_target="tpu_custom_call" | custom-call | tf_op jit(solution)/shard_map/pallas_call | solution.py:325
  33.1 16.4 %all_to_all.5 = bf16[16,56,128]{2,1,0:T(8,128)(2,1)S(1)} all-to-all(bf16[16,56,128]{2,1,0:T(8,128)(2,1)S(1)} %bitcast.15), channel_id=1, replica_groups={{0,2,4,6,8,10,12,14,16,18,20,22,24,26,28,30},{1,3,5,7,9,11,13,15,17,19,..., dimensions={0} | all-to-all | bytes 458752 | tf_op jit(solution)/shard_map/all_to_all | solution.py:344
  49.5 0.8 %finish.1 = f32[3,64,129]{2,1,0:T(8,128)} custom-call(bf16[4,4,56,128]{3,2,1,0:T(8,128)(2,1)S(1)} %bitcast.14), custom_call_target="tpu_custom_call" | custom-call | tf_op jit(solution)/shard_map/finish/pallas_call | solution.py:352
  (10 shorter events, 0.0 us)
Async XLA Ops:
  0.0 8.8 %copy-start.6 = (s32[2,4]{1,0:T(2,128)S(1)}, s32[2,4]{1,0:T(2,128)}, u32[]{:S(2)}) copy-start(s32[2,4]{1,0:T(2,128)} %valid.7) | copy-start | bytes 100
  0.0 24.1 %copy-start = (bf16[1024,1024]{1,0:T(8,128)(2,1)S(1)}, bf16[1024,1024]{1,0:T(8,128)(2,1)}, u32[]{:S(2)}) copy-start(bf16[1024,1024]{1,0:T(8,128)(2,1)} %constant.11.refs_4_.refs_3_) | copy-start | bytes 6291460
  1.1 11.1 %collective-permute-start.5 = (bf16[2,64,1024]{2,1,0:T(8,128)(2,1)S(1)}, bf16[2,64,1024]{2,1,0:T(8,128)(2,1)S(1)}, u32[]{:S(2)}, u32[]{:S(2)}) collective-permute-start(bf16[2,64,1024]{2,1,0:T(8,128)(2,1)S(1)} %bitcast.16), channel_id=1, source_target_pairs={{0,24},{1,25},{2,26},{3,27},{4,28},{5,29},{6,30},{7,31},{8,16},{9,... | collective-permute-start | bytes 786440 | tf_op jit(solution)/shard_map/ppermute | solution.py:277
  6.6 10.9 %collective-permute-start.6 = (bf16[2,64,1024]{2,1,0:T(8,128)(2,1)S(1)}, bf16[2,64,1024]{2,1,0:T(8,128)(2,1)S(1)}, u32[]{:S(2)}, u32[]{:S(2)}) collective-permute-start(bf16[2,64,1024]{2,1,0:T(8,128)(2,1)S(1)} %bitcast.21), channel_id=1, source_target_pairs={{0,25},{1,24},{2,27},{3,26},{4,29},{5,28},{6,31},{7,30},{8,17},{9,... | collective-permute-start | bytes 786440 | tf_op jit(solution)/shard_map/ppermute | solution.py:277
  6.7 12.7 %collective-permute-start.7 = (bf16[2,64,1024]{2,1,0:T(8,128)(2,1)S(1)}, bf16[2,64,1024]{2,1,0:T(8,128)(2,1)S(1)}, u32[]{:S(2)}, u32[]{:S(2)}) collective-permute-start(bf16[2,64,1024]{2,1,0:T(8,128)(2,1)S(1)} %bitcast.20), channel_id=1, source_target_pairs={{0,1},{1,0},{2,3},{3,2},{4,5},{5,4},{6,7},{7,6},{8,9},{9,8},{10,11... | collective-permute-start | bytes 786440 | tf_op jit(solution)/shard_map/ppermute | solution.py:277
  6.8 17.2 %collective-permute-start.8 = (bf16[2,64,1024]{2,1,0:T(8,128)(2,1)S(1)}, bf16[2,64,1024]{2,1,0:T(8,128)(2,1)S(1)}, u32[]{:S(2)}, u32[]{:S(2)}) collective-permute-start(bf16[2,64,1024]{2,1,0:T(8,128)(2,1)S(1)} %bitcast.19), channel_id=1, source_target_pairs={{0,8},{1,9},{2,10},{3,11},{4,12},{5,13},{6,14},{7,15},{8,0},{9,1},... | collective-permute-start | bytes 786440 | tf_op jit(solution)/shard_map/ppermute | solution.py:277
  8.8 1.2 %collective-permute-start = (s32[2,4]{1,0:T(2,128)S(1)}, s32[2,4]{1,0:T(2,128)S(1)}, u32[]{:S(2)}, u32[]{:S(2)}) collective-permute-start(s32[2,4]{1,0:T(2,128)S(1)} %copy-done.6), channel_id=1, source_target_pairs={{0,1},{1,0},{2,3},{3,2},{4,5},{5,4},{6,7},{7,6},{8,9},{9,8},{10,11... | collective-permute-start | bytes 104 | tf_op jit(solution)/shard_map/ppermute | solution.py:283
  9.9 16.3 %collective-permute-start.9 = (bf16[2,64,1024]{2,1,0:T(8,128)(2,1)S(1)}, bf16[2,64,1024]{2,1,0:T(8,128)(2,1)S(1)}, u32[]{:S(2)}, u32[]{:S(2)}) collective-permute-start(bf16[2,64,1024]{2,1,0:T(8,128)(2,1)S(1)} %bitcast.18), channel_id=1, source_target_pairs={{0,16},{1,17},{2,18},{3,19},{4,20},{5,21},{6,22},{7,23},{8,24},{9,... | collective-permute-start | bytes 786440 | tf_op jit(solution)/shard_map/ppermute | solution.py:277
  12.3 16.1 %collective-permute-start.3 = (bf16[2,32,1024]{2,1,0:T(8,128)(2,1)S(1)}, bf16[2,32,1024]{2,1,0:T(8,128)(2,1)S(1)}, u32[]{:S(2)}, u32[]{:S(2)}) collective-permute-start(bf16[2,32,1024]{2,1,0:T(8,128)(2,1)S(1)} %bitcast.25), channel_id=1, source_target_pairs={{0,9},{1,8},{2,11},{3,10},{4,13},{5,12},{6,15},{7,14},{8,1},{9,0},... | collective-permute-start | bytes 393224 | tf_op jit(solution)/shard_map/ppermute | solution.py:277
  17.5 10.9 %collective-permute-start.4 = (bf16[2,32,1024]{2,1,0:T(8,128)(2,1)S(1)}, bf16[2,32,1024]{2,1,0:T(8,128)(2,1)S(1)}, u32[]{:S(2)}, u32[]{:S(2)}) collective-permute-start(bf16[2,32,1024]{2,1,0:T(8,128)(2,1)S(1)} %bitcast.24), channel_id=1, source_target_pairs={{0,17},{1,16},{2,19},{3,18},{4,21},{5,20},{6,23},{7,22},{8,25},{9,... | collective-permute-start | bytes 393224 | tf_op jit(solution)/shard_map/ppermute | solution.py:277
  19.3 11.4 %collective-permute-start.2 = (bf16[2,32,1024]{2,1,0:T(8,128)(2,1)S(1)}, bf16[2,32,1024]{2,1,0:T(8,128)(2,1)S(1)}, u32[]{:S(2)}, u32[]{:S(2)}) collective-permute-start(bf16[2,32,1024]{2,1,0:T(8,128)(2,1)S(1)} %bitcast.23), channel_id=1, source_target_pairs={{0,17},{1,16},{2,19},{3,18},{4,21},{5,20},{6,23},{7,22},{8,25},{9,... | collective-permute-start | bytes 393224 | tf_op jit(solution)/shard_map/ppermute | solution.py:277
  24.1 6.7 %collective-permute-start.1 = (bf16[2,32,1024]{2,1,0:T(8,128)(2,1)S(1)}, bf16[2,32,1024]{2,1,0:T(8,128)(2,1)S(1)}, u32[]{:S(2)}, u32[]{:S(2)}) collective-permute-start(bf16[2,32,1024]{2,1,0:T(8,128)(2,1)S(1)} %bitcast.22), channel_id=1, source_target_pairs={{0,9},{1,8},{2,11},{3,10},{4,13},{5,12},{6,15},{7,14},{8,1},{9,0},... | collective-permute-start | bytes 393224 | tf_op jit(solution)/shard_map/ppermute | solution.py:277
  24.1 2.2 %copy-start.5 = (s32[3,4]{1,0:T(4,128)S(1)}, s32[3,4]{1,0:T(4,128)}, u32[]{:S(2)}) copy-start(s32[3,4]{1,0:T(4,128)} %plan.5) | copy-start | bytes 148
  26.2 2.2 %copy-start.1 = (bf16[1024,256]{1,0:T(8,128)(2,1)S(1)}, bf16[1024,256]{1,0:T(8,128)(2,1)}, u32[]{:S(2)}) copy-start(bf16[1024,256]{1,0:T(8,128)(2,1)} %constant.15.refs_6_.refs_7_) | copy-start | bytes 1572868
  26.2 2.2 %copy-start.2 = (bf16[1024,256]{1,0:T(8,128)(2,1)S(1)}, bf16[1024,256]{1,0:T(8,128)(2,1)}, u32[]{:S(2)}) copy-start(bf16[1024,256]{1,0:T(8,128)(2,1)} %constant.12.refs_5_.refs_6_) | copy-start | bytes 1572868
  26.2 2.2 %copy-start.3 = (bf16[16,1024]{1,0:T(8,128)(2,1)S(1)}, bf16[16,1024]{1,0:T(8,128)(2,1)}, u32[]{:S(2)}) copy-start(bf16[16,1024]{1,0:T(8,128)(2,1)} %constant.19.refs_8_.refs_9_) | copy-start | bytes 98308
  26.2 2.2 %copy-start.4 = (bf16[16,1024]{1,0:T(8,128)(2,1)S(1)}, bf16[16,1024]{1,0:T(8,128)(2,1)}, u32[]{:S(2)}) copy-start(bf16[16,1024]{1,0:T(8,128)(2,1)} %constant.16.refs_7_.refs_8_) | copy-start | bytes 98308
where the time goes:
time: 50.5 us; the launch traced here: 50.3 us
  blocking collectives  16.4 us (32%)
  Pallas kernels  12.2 us (24%)
  waiting for transfers between devices  11.9 us (24%)
  starting transfers between devices  9.57 us (19%)
    all_to_all x1, blocking collectives, by_channels(): lax.all_to_all(sent.reshape(chan_count * zones, height, LANES), ('chan',...  16.4 us
    ppermute x9, waiting for transfers between devices, by_channels(): piece = lax.ppermute(piece, ('chan', 'tm'), partners(*key))  10.7 us
    ppermute x9, starting transfers between devices, by_channels(): piece = lax.ppermute(piece, ('chan', 'tm'), partners(*key))  9.57 us
    pallas_call x2, Pallas kernels, by_channels(): pl.pallas_call(functools.partial(second_kernel, rounds, early_slots, late...  4.62 us
    pallas_call x2, Pallas kernels, cut(): pl.pallas_call(functools.partial(cut_kernel, keys, zone_ranges), out_shap...  2.6 us
    pallas_call x1, Pallas kernels, by_channels(): pl.pallas_call(functools.partial(early_kernel, early_slots), out_shape=ja...  2.11 us
    pallas_call x1, Pallas kernels, by_channels(): pl.pallas_call(functools.partial(first_kernel, early_slots, late_steps),...  2.1 us
    ppermute x1, waiting for transfers between devices, by_channels(): other = lax.ppermute(valid, ('chan', 'tm'), partners(1, 0))  1.16 us
  transfers between devices with their start and end apart: 10, of which 4 were waited for; matrix products, arithmetic and copies ran while one was open for 0% of the time, Pallas kernels for 16%

commit v1 on v0

--- a/solution.py
+++ b/solution.py
@@ -40,38 +40,61 @@
     return high, (value - high.astype(jnp.float32)).astype(jnp.bfloat16)
 
 
-def whiten(pieces, masks, table, spec, white):
-    windows, rows, length = pieces[0][2].shape
+def whiten(pieces, table, spec):
+    length = pieces[0][0].shape[2]
     bins = length // 2
-    data = jnp.concatenate([piece[...].reshape(windows * rows, length) for _, _, piece in pieces], axis=0)
+    data = jnp.concatenate([piece[...].reshape(-1, length) for piece, _, _ in pieces], axis=0)
     spec[: data.shape[0], :] = jnp.dot(data, table[...], preferred_element_type=jnp.float32)
-    for order, (half, slot, _) in enumerate(pieces):
+    start = 0
+    for piece, target, present in pieces:
+        windows, rows, _ = piece.shape
         for window in range(windows):
-            present = masks[half][window, lax.axis_index("chan") ^ slot].astype(jnp.float32)
-            start = (order * windows + window) * rows
-
-            def body(step, carry):
-                row = pl.multiple_of(step * STEP, STEP)
-                real = spec[pl.ds(start + row, STEP), :bins]
-                imag = spec[pl.ds(start + row, STEP), bins:]
+            keep = present(window).astype(jnp.float32)
+            for row in range(0, rows, STEP):
+                real = spec[start + row : start + row + STEP, :bins]
+                imag = spec[start + row : start + row + STEP, bins:]
                 power = real * real + imag * imag
                 level = jnp.mean(power, axis=1, keepdims=True)
-                scale = lax.rsqrt(power + 0.1 * level + 1e-06) * present
-                target = white(half, slot)
-                target[window, pl.ds(row, STEP), :bins] = (real * scale).astype(jnp.bfloat16)
-                target[window, pl.ds(row, STEP), bins:] = (imag * scale).astype(jnp.bfloat16)
-                return carry
-
-            lax.fori_loop(0, rows // STEP, body, 0, unroll=True)
-
-
-def cross(white, first, second, row, rows):
-    bins = white.shape[3] // 2
-    real_sum, imag_sum = None, None
-    for window in range(white.shape[1]):
-        own = white[first, window, pl.ds(row, rows), :].astype(jnp.float32)
-        other = white[second, window, pl.ds(row, rows), :].astype(jnp.float32)
-        own_re, own_im, other_re, other_im = own[:, :bins], own[:, bins:], other[:, :bins], other[:, bins:]
+                scale = lax.rsqrt(power + 0.1 * level + 1e-06) * keep
+                target[window, row : row + STEP, :bins] = (real * scale).astype(jnp.bfloat16)
+                target[window, row : row + STEP, bins:] = (imag * scale).astype(jnp.bfloat16)
+            start += rows
+
+
+def sent_kernel(count, valid, *refs):
+    pieces, table, outs, spec = refs[:count], refs[count], refs[count + 1 : -1], refs[-1]
+    here = lax.axis_index("chan")
+    whiten([(piece, out, lambda window: valid[window, here]) for piece, out in zip(pieces, outs, strict=True)], table, spec)
+
+
+def early_kernel(slots, valid, other, *refs):
+    pieces, (table, out, spec) = refs[:-3], refs[-3:]
+    here = lax.axis_index("chan")
+    listed = []
+    for order, ((half, slot), piece) in enumerate(zip(slots, pieces, strict=True)):
+        mask = (valid, other)[half]
+        listed.append((piece, out.at[order], lambda window, mask=mask, slot=slot: mask[window, here ^ slot]))
+    whiten(listed, table, spec)
+
+
+def slot_pairs(slots):
+    return [(first, second) for first in range(slots) for second in range(first + 1, slots)]
+
+
+def load_slots(sources, row, lane, bins):
+    values = {}
+    for slot, (ref, base) in sources.items():
+        for window in range(ref.shape[0]):
+            rows = slice(base + row, base + row + STEP)
+            real = ref[window, rows, lane : lane + LANES].astype(jnp.float32)
+            imag = ref[window, rows, bins + lane : bins + lane + LANES].astype(jnp.float32)
+            values[slot, window] = (real, imag)
+    return values
+
+
+def cross(values, windows, first, second, real_sum=None, imag_sum=None):
+    for window in range(windows):
+        (own_re, own_im), (other_re, other_im) = values[first, window], values[second, window]
         real_part = own_re * other_re + own_im * other_im
         imag_part = own_im * other_re - own_re * other_im
         real_sum = real_part if real_sum is None else real_sum + real_part
@@ -79,108 +102,81 @@
     return real_sum, imag_sum
 
 
-def list_pairs(plan, lead, mate):
-    rounds, blocks = plan.shape
-    place = 0
-    for step in range(rounds):
-        place = step * (blocks // 2)
-        for block in range(blocks):
-            partner = plan[step, block]
-            lead[place] = block
-            mate[place] = partner
-            place = place + (partner > block).astype(jnp.int32)
-
-
-def early_kernel(slots, valid, other, *refs):
-    pieces, (table, out, spec) = refs[:-3], refs[-3:]
-    place = {key: order for order, key in enumerate(slots)}
-    listed = [(half, slot, piece) for (half, slot), piece in zip(slots, pieces, strict=True)]
-    whiten(listed, (valid, other), table, spec, lambda half, slot: out.at[place[half, slot]])
-
-
-def gather_white(half, slots, late, early, white):
-    for order, (early_half, slot) in enumerate(slots):
-        if early_half == half:
-            white[slot] = early[order]
-    return [(half, slot, piece) for slot, piece in late]
-
-
-def first_kernel(slots, late, plan, valid, other, *refs):
-    pieces, (early, table, stack, spec, white, lead, mate) = refs[:-7], refs[-7:]
-    here = lax.axis_index("chan")
-    list_pairs(plan, lead, mate)
-    listed = gather_white(0, slots, list(zip(late, pieces, strict=True)), early, white)
-    whiten(listed, (valid, other), table, spec, lambda half, slot: white.at[slot])
-    pairs, rows, width = stack.shape
+def first_kernel(early_slots, late, *refs):
+    pieces, early, stack = refs[: len(late)], refs[len(late)], refs[len(late) + 1]
+    sources = {slot: (piece, 0) for slot, piece in zip(late, pieces, strict=True)}
+    sources.update({slot: (early.at[order], 0) for order, (half, slot) in enumerate(early_slots) if half == 0})
+    ready = {slot: (early.at[order], 0) for order, (half, slot) in enumerate(early_slots) if half == 1}
+    windows = early.shape[1]
+    _, rows, width = stack.shape
     bins = width // 2
-    for pair in range(pairs):
-        first, second = lead[pair] ^ here, mate[pair] ^ here
-
-        def body(step, carry):
-            row = pl.multiple_of(step * STEP, STEP)
-            real_sum, imag_sum = cross(white, first, second, row, STEP)
-            stack[pair, pl.ds(row, STEP), :bins] = real_sum
-            stack[pair, pl.ds(row, STEP), bins:] = imag_sum
-            return carry
-
-        lax.fori_loop(0, rows // STEP, body, 0, unroll=True)
-
-
-def second_kernel(rounds, slots, late, part, plan, valid, other, *refs):
+    for row in range(0, rows, STEP):
+        for lane in range(0, bins, LANES):
+            values = load_slots(sources, row, lane, bins)
+            more = load_slots(ready, row, lane, bins)
+            for pair, (first, second) in enumerate(slot_pairs(len(sources))):
+                sums = cross(values, windows, first, second)
+                if first in ready and second in ready:
+                    sums = cross(more, windows, first, second, *sums)
+                stack[pair, row : row + STEP, lane : lane + LANES] = sums[0]
+                stack[pair, row : row + STEP, bins + lane : bins + lane + LANES] = sums[1]
+
+
+def second_kernel(rounds, early_slots, late, part, plan, valid, other, *refs):
     head, refs = refs[: len(late)], refs[len(late) :]
     done, refs = refs[:part], refs[part:]
-    early, table, stack, lag_hi, lag_lo, end_hi, end_lo, out, spec, white, hi, lo, main, extra, lead, mate = refs
+    early, stack, lag_hi, lag_lo, out, both, main, extra = refs
     here = lax.axis_index("chan")
-    list_pairs(plan, lead, mate)
-    rows = head[0].shape[1]
+    windows, rows, width = head[0].shape
     base = part * rows
-    for order, (half, slot) in enumerate(slots):
-        if half == 1:
-            white[slot] = early[order, :, base : base + rows, :]
-    whiten([(1, slot, piece) for slot, piece in zip(late, head, strict=True)], (valid, other), table, spec, lambda half, slot: white.at[slot])
-    pairs, _, width = stack.shape
     bins = width // 2
-    for pair in range(pairs):
-        first, second = lead[pair] ^ here, mate[pair] ^ here
-
-        def body(step, carry):
-            row = pl.multiple_of(step * STEP, STEP)
-            real_sum, imag_sum = cross(white, first, second, row, STEP)
-            real_sum = real_sum + stack[pair, pl.ds(base + row, STEP), :bins]
-            imag_sum = imag_sum + stack[pair, pl.ds(base + row, STEP), bins:]
-            place = pl.ds(pl.multiple_of(pair * rows + row, STEP), STEP)
-            hi[place, :bins], lo[place, :bins] = split(real_sum)
-            hi[place, bins:], lo[place, bins:] = split(imag_sum)
-            return carry
-
-        lax.fori_loop(0, rows // STEP, body, 0, unroll=True)
+    ready = {slot: (early.at[order], base) for order, (half, slot) in enumerate(early_slots) if half == 1}
+    sources = {slot: (piece, 0) for slot, piece in zip(late, head, strict=True)}
+    sources.update(ready)
+    pairs = slot_pairs(len(sources))
+    height = len(pairs) * rows
+    for row in range(0, rows, STEP):
+        for lane in range(0, bins, LANES):
+            values = load_slots(sources, row, lane, bins)
+            for pair, (first, second) in enumerate(pairs):
+                lanes = (slice(lane, lane + LANES), slice(bins + lane, bins + lane + LANES))
+                sums = [stack[pair, base + row : base + row + STEP, where] for where in lanes]
+                if not (first in ready and second in ready):
+                    sums = cross(values, windows, first, second, *sums)
+                start = pair * rows + row
+                for where, value in zip(lanes, sums, strict=True):
+                    high, low = split(value)
+                    both[start : start + STEP, where] = high
+                    both[height + start : height + start + STEP, where] = low
     dot = functools.partial(jnp.dot, preferred_element_type=jnp.float32)
-    main[...] = dot(hi[...], lag_hi[...]) + dot(lo[...], lag_hi[...]) + dot(hi[...], lag_lo[...])
-    across = functools.partial(
-        lax.dot_general, dimension_numbers=(((1,), (1,)), ((), ())), preferred_element_type=jnp.float32
-    )
-    ends = across(end_hi[...], hi[...]) + across(end_hi[...], lo[...]) + across(end_lo[...], hi[...])
+    double = dot(both[...], lag_hi[...])
+    main[...] = double[:height] + double[height:] + dot(both[:height, :], lag_lo[...])
     extra[...] = jnp.zeros_like(extra)
     group = (out.shape[2] - 8) // rounds
     zones = rows // group
     for earlier, ref in enumerate(done):
         out[:, earlier * zones : (earlier + 1) * zones] = ref[:, earlier * zones : (earlier + 1) * zones]
     first_zone = part * zones
-    per_round = pairs // rounds
-    for pair in range(pairs):
-        step = pair // per_round
+    diagonal = lax.broadcasted_iota(jnp.int32, (rows, LANES), 0) == lax.broadcasted_iota(jnp.int32, (rows, LANES), 1)
+    for pair, slots in enumerate(pairs):
+        blocks = [slot ^ here for slot in slots]
+        step = 0
+        for turn in range(1, rounds):
+            step = step + turn * (plan[turn, blocks[0]] == blocks[1]).astype(jnp.int32)
         count = 0
         for mask in (valid, other):
             for window in range(mask.shape[0]):
-                count = count + mask[window, lead[pair]] * mask[window, mate[pair]]
+                count = count + mask[window, blocks[0]] * mask[window, blocks[1]]
         count = jnp.full((1, LANES), count.astype(jnp.float32))
+        place = pl.ds(pl.multiple_of(step * group, group), group)
         for side in range(2):
-            block = (lead, mate)[side][pair]
-            extra[block, rounds + step : rounds + step + 1, :] = count
             value = main[pair * rows : (pair + 1) * rows, side * LANES : (side + 1) * LANES]
             value = value.astype(jnp.bfloat16).reshape(zones, group, LANES)
-            out[block, first_zone : first_zone + zones, step * group : (step + 1) * group, :] = value
-            extra[block, step : step + 1, :rows] = ends[side : side + 1, pair * rows : (pair + 1) * rows]
+            out[blocks[side], first_zone : first_zone + zones, place, :] = value
+            mirror = main[pair * rows : (pair + 1) * rows, (1 - side) * LANES : (1 - side) * LANES + 1]
+            end = jnp.sum(jnp.where(diagonal, mirror, 0.0), axis=0, keepdims=True)
+            extra[blocks[side], pl.ds(step, 1), :] = end
+            extra[blocks[side], pl.ds(rounds + step, 1), :] = count
     for block in range(out.shape[0]):
         tail = extra[block].astype(jnp.bfloat16)
         for zone in range(zones):
@@ -271,8 +267,19 @@
     ranges += [(part * per_part, per_part) for part in range(PARTS) for _ in late_second]
     pieces = cut(keys[:1], ranges[:1])
     pieces += cut(keys[1:], ranges[1:])
+    table = jnp.asarray(dft_table(length, bins).astype(np.float32)).astype(jnp.bfloat16)
+    raw, late_raw = pieces[: len(early_slots)], pieces[len(early_slots) :]
+    late_white = pl.pallas_call(
+        functools.partial(sent_kernel, len(late_raw)),
+        out_shape=[jax.ShapeDtypeStruct(piece.shape, jnp.bfloat16) for piece in late_raw],
+        in_specs=[smem] + [vmem] * (len(late_raw) + 1),
+        out_specs=[vmem] * len(late_raw),
+        scratch_shapes=[pltpu.VMEM((2 * len(late_steps) * windows * rows, length), jnp.float32)],
+        compiler_params=params,
+        name="whiten_sent",
+    )(valid, *late_raw, table)
     received, sent_pieces = [], 0
-    for key, piece in zip(keys, pieces, strict=True):
+    for key, piece in zip(keys, [*raw, *late_white], strict=True):
         if key != (0, 0):
             piece = lax.ppermute(piece, ("chan", "tm"), partners(*key))
             sent_pieces += 1
@@ -281,41 +288,28 @@
     first_pieces, second_pieces = received[: len(late_steps)], received[len(late_steps) :]
 
     other = lax.ppermute(valid, ("chan", "tm"), partners(1, 0))
-    pairs = rounds * (chan_count // 2)
-    table = jnp.asarray(dft_table(length, bins).astype(np.float32)).astype(jnp.bfloat16)
+    pairs = len(slot_pairs(chan_count))
     shifts = np.arange(-maxlag, maxlag, dtype=np.int64)
     lags = np.concatenate([lag_table(bins, length, shifts, s) for s in (1.0, -1.0)], axis=1)
     lag_hi, lag_lo = high_low(lags)
-    last = np.array([maxlag], dtype=np.int64)
-    ends = np.concatenate([lag_table(bins, length, last, s) for s in (1.0, -1.0)], axis=1).T
-    end_hi, end_lo = high_low(np.pad(ends, ((0, 14), (0, 0))))
-
-    lists = [pltpu.SMEM((pairs + 1,), jnp.int32)] * 2
-
-    def spec_scratch(pieces, height):
-        return pltpu.VMEM((pieces * windows * height, length), jnp.float32)
-
-    def white_scratch(height):
-        return pltpu.VMEM((chan_count, windows, height, length), jnp.bfloat16)
 
     early = pl.pallas_call(
         functools.partial(early_kernel, early_slots),
         out_shape=jax.ShapeDtypeStruct((len(early_slots), windows, rows, length), jnp.bfloat16),
         in_specs=[smem] * 2 + [vmem] * (len(early_slots) + 1),
         out_specs=vmem,
-        scratch_shapes=[spec_scratch(len(early_slots), rows)],
+        scratch_shapes=[pltpu.VMEM((len(early_slots) * windows * rows, length), jnp.float32)],
         compiler_params=params,
         name="early",
     )(valid, other, *early_pieces, table)
     stack = pl.pallas_call(
         functools.partial(first_kernel, early_slots, late_steps),
         out_shape=jax.ShapeDtypeStruct((pairs, rows, length), jnp.float32),
-        in_specs=[smem] * 3 + [vmem] * (len(late_steps) + 2),
+        in_specs=[vmem] * (len(late_steps) + 1),
         out_specs=vmem,
-        scratch_shapes=[spec_scratch(len(late_steps), rows), white_scratch(rows), *lists],
         compiler_params=params,
         name="first_half",
-    )(plan, valid, other, *first_pieces, early, table)
+    )(*first_pieces, early)
     height = rounds * group + 8
     part_rows = per_part * group
     sent = []
@@ -325,19 +319,15 @@
             pl.pallas_call(
                 functools.partial(second_kernel, rounds, early_slots, late_steps, part),
                 out_shape=jax.ShapeDtypeStruct((chan_count, zones, height, LANES), jnp.bfloat16),
-                in_specs=[smem] * 3 + [vmem] * (len(late_steps) + part + 7),
+                in_specs=[smem] * 3 + [vmem] * (len(late_steps) + part + 4),
                 out_specs=vmem,
                 scratch_shapes=[
-                    spec_scratch(len(late_steps), part_rows),
-                    white_scratch(part_rows),
-                    pltpu.VMEM((pairs * part_rows, length), jnp.bfloat16),
-                    pltpu.VMEM((pairs * part_rows, length), jnp.bfloat16),
+                    pltpu.VMEM((2 * pairs * part_rows, length), jnp.bfloat16),
                     pltpu.VMEM((pairs * part_rows, 2 * LANES), jnp.float32),
                     pltpu.VMEM((chan_count, 8, LANES), jnp.float32),
-                    *lists,
                 ],
                 compiler_params=params,
-            )(plan, valid, other, *heads, *sent, early, table, stack, lag_hi, lag_lo, end_hi, end_lo)
+            )(plan, valid, other, *heads, *sent, early, stack, lag_hi, lag_lo)
         )
     sent = sent[-1]
     same_half = [[a * time_count + z * 2 + c for a in range(chan_count) for z in range(zones)] for c in range(2)]
@@ -424,7 +414,7 @@
     block_width = samples.shape[1]
     rows_each = block_width // (time_count * chan_count)
     whole_tiles = rows_each > 0 and rows_each % STEP == 0 and block_width == rows_each * time_count * chan_count
-    whole_tiles = whole_tiles and time_count % (2 * PARTS) == 0
+    whole_tiles = whole_tiles and time_count % (2 * PARTS) == 0 and plan.shape[0] == chan_count - 1
     powers = chan_count & (chan_count - 1) == 0 and chan_count > 1 and time_count % 2 == 0
     if whole_tiles and powers and rows_each * time_count // 2 <= LANES and 2 * plan.shape[0] <= 8:
         return by_channels(samples, valid, plan)

time: 50.5 us -> 49.9 us (0.988)
  Pallas kernels: 12.2 us -> 11 us
  waiting for transfers between devices: 11.9 us -> 12.6 us
    pallas_call x0 -> x1, Pallas kernels: none -> 2.11 us  [by_channels(): pl.pallas_call(functools.partial(sent_kernel, len(late_raw)), out_shape=[...]
    pallas_call x2, Pallas kernels: 4.62 us -> 2.8 us  [by_channels(): pl.pallas_call(functools.partial(second_kernel, rounds, early_slots, late...]
    pallas_call x1, Pallas kernels: 2.1 us -> 0.54 us  [by_channels(): pl.pallas_call(functools.partial(first_kernel, early_slots, late_steps),...]
    ppermute x9, waiting for transfers between devices: 10.7 us -> 11.5 us  [by_channels(): piece = lax.ppermute(piece, ('chan', 'tm'), partners(*key))]
  transfers between devices with their start and end apart: 10 -> 10, of which waited for: 4 -> 5; matrix products, arithmetic and copies ran while one was open for 0% -> 0% of each run, Pallas kernels for 16% -> 15%
where the time goes in v1:
time: 49.9 us; the launch traced here: 49.7 us
  blocking collectives  16.2 us (32%)
  waiting for transfers between devices  12.6 us (25%)
  Pallas kernels  11 us (22%)
  starting transfers between devices  9.75 us (20%)
    all_to_all x1, blocking collectives, by_channels(): lax.all_to_all(sent.reshape(chan_count * zones, height, LANES), ('chan',...  16.2 us
    ppermute x9, waiting for transfers between devices, by_channels(): piece = lax.ppermute(piece, ('chan', 'tm'), partners(*key))  11.5 us
    ppermute x9, starting transfers between devices, by_channels(): piece = lax.ppermute(piece, ('chan', 'tm'), partners(*key))  9.74 us
    pallas_call x2, Pallas kernels, by_channels(): pl.pallas_call(functools.partial(second_kernel, rounds, early_slots, late...  2.8 us
    pallas_call x2, Pallas kernels, cut(): pl.pallas_call(functools.partial(cut_kernel, keys, zone_ranges), out_shap...  2.6 us
    pallas_call x1, Pallas kernels, by_channels(): pl.pallas_call(functools.partial(sent_kernel, len(late_raw)), out_shape=[...  2.11 us
    pallas_call x1, Pallas kernels, by_channels(): pl.pallas_call(functools.partial(early_kernel, early_slots), out_shape=ja...  2.11 us
    ppermute x1, waiting for transfers between devices, by_channels(): other = lax.ppermute(valid, ('chan', 'tm'), partners(1, 0))  1.16 us
  transfers between devices with their start and end apart: 10, of which 5 were waited for; matrix products, arithmetic and copies ran while one was open for 0% of the time, Pallas kernels for 15%

profile of v1, /device:TPU:0, one launch (start us, length us, event | category | flops | bytes accessed | tf_op | source)
XLA Modules:
  0.0 49.7 jit_solution(11856639442549728060)
XLA Ops:
  0.0 1.1 %shard_map.65 = bf16[2,4,16,1024]{3,2,1,0:T(8,128)(2,1)S(1)} custom-call(bf16[2,4,2,4,16,1024]{5,4,3,2,1,0:T(8,128)(2,1)} %bitcast.26), custom_call_target="tpu_custom_call" | custom-call | tf_op jit(solution)/shard_map/pallas_call | solution.py:237
  1.1 4.0 %collective-permute-start.5 = (bf16[2,64,1024]{2,1,0:T(8,128)(2,1)S(1)}, bf16[2,64,1024]{2,1,0:T(8,128)(2,1)S(1)}, u32[]{:S(2)}, u32[]{:S(2)}) collective-permute-start(bf16[2,64,1024]{2,1,0:T(8,128)(2,1)S(1)} %bitcast.16), channel_id=1, source_target_pairs={{0,24},{1,25},{2,26},{3,27},{4,28},{5,29},{6,30},{7,31},{8,16},{9,... | collective-permute-start | bytes 786440 | tf_op jit(solution)/shard_map/ppermute | solution.py:284
  5.1 1.5 %shard_map.64 = (bf16[2,4,16,1024]{3,2,1,0:T(8,128)(2,1)S(1)}, bf16[2,4,16,1024]{3,2,1,0:T(8,128)(2,1)S(1)}, bf16[2,4,16,1024]{3,2,1,0:T(8,128)(2,1)S(1)}, bf16[...) custom-call(bf16[2,4,2,4,16,1024]{5,4,3,2,1,0:T(8,128)(2,1)} %bitcast.27), custom_call_target="tpu_custom_call" | custom-call | tf_op jit(solution)/shard_map/pallas_call | solution.py:237
  6.6 2.1 %whiten_sent.1 = (bf16[2,64,1024]{2,1,0:T(8,128)(2,1)S(1)}, bf16[2,64,1024]{2,1,0:T(8,128)(2,1)S(1)}, bf16[2,32,1024]{2,1,0:T(8,128)(2,1)S(1)}, bf16[2,32,1024]{...) custom-call(s32[2,4]{1,0:T(2,128)S(1)} %copy-done.3, ...), custom_call_target="tpu_custom_call" | custom-call | tf_op jit(solution)/shard_map/whiten_sent/pallas_call | solution.py:272
  8.7 0.6 %collective-permute-start.8 = (bf16[2,64,1024]{2,1,0:T(8,128)(2,1)S(1)}, bf16[2,64,1024]{2,1,0:T(8,128)(2,1)S(1)}, u32[]{:S(2)}, u32[]{:S(2)}) collective-permute-start(bf16[2,64,1024]{2,1,0:T(8,128)(2,1)S(1)} %get-tuple-element.33), channel_id=1, source_target_pairs={{0,8},{1,9},{2,10},{3,11},{4,12},{5,13},{6,14},{7,15},{8,0},{9,1},... | collective-permute-start | bytes 786440 | tf_op jit(solution)/shard_map/ppermute | solution.py:284
  9.3 0.3 collective-permute-start.6
  9.7 1.2 %collective-permute-start.7 = (bf16[2,64,1024]{2,1,0:T(8,128)(2,1)S(1)}, bf16[2,64,1024]{2,1,0:T(8,128)(2,1)S(1)}, u32[]{:S(2)}, u32[]{:S(2)}) collective-permute-start(bf16[2,64,1024]{2,1,0:T(8,128)(2,1)S(1)} %bitcast.24), channel_id=1, source_target_pairs={{0,1},{1,0},{2,3},{3,2},{4,5},{5,4},{6,7},{7,6},{8,9},{9,8},{10,11... | collective-permute-start | bytes 786440 | tf_op jit(solution)/shard_map/ppermute | solution.py:284
  10.9 0.0 collective-permute-start
  10.9 1.2 %collective-permute-done.other = s32[2,4]{1,0:T(2,128)S(1)} collective-permute-done((s32[2,4]{1,0:T(2,128)S(1)}, s32[2,4]{1,0:T(2,128)S(1)}, u32[]{:S(2)}, u32[]{:S(2)}) %collective-permute-start) | collective-permute-done | bytes 64 | tf_op jit(solution)/shard_map/ppermute | solution.py:290
  12.1 1.5 %collective-permute-start.9 = (bf16[2,64,1024]{2,1,0:T(8,128)(2,1)S(1)}, bf16[2,64,1024]{2,1,0:T(8,128)(2,1)S(1)}, u32[]{:S(2)}, u32[]{:S(2)}) collective-permute-start(bf16[2,64,1024]{2,1,0:T(8,128)(2,1)S(1)} %get-tuple-element.34), channel_id=1, source_target_pairs={{0,16},{1,17},{2,18},{3,19},{4,20},{5,21},{6,22},{7,23},{8,24},{9,... | collective-permute-start | bytes 786440 | tf_op jit(solution)/shard_map/ppermute | solution.py:284
  13.6 0.0 collective-permute-done.5.refs_0_
  13.6 0.2 collective-permute-start.3
  13.8 4.2 %collective-permute-done.8.refs_0_ = bf16[2,64,1024]{2,1,0:T(8,128)(2,1)S(1)} collective-permute-done((bf16[2,64,1024]{2,1,0:T(8,128)(2,1)S(1)}, bf16[2,64,1024]{2,1,0:T(8,128)(2,1)S(1)}, u32[]{:S(2)}, u32[]{:S(2)}) %collective-permute-start.8) | collective-permute-done | bytes 262176 | tf_op jit(solution)/shard_map/ppermute | solution.py:284
  18.0 0.0 collective-permute-start.4
  18.0 5.1 %collective-permute-done.6.refs_1_ = bf16[2,64,1024]{2,1,0:T(8,128)(2,1)S(1)} collective-permute-done((bf16[2,64,1024]{2,1,0:T(8,128)(2,1)S(1)}, bf16[2,64,1024]{2,1,0:T(8,128)(2,1)S(1)}, u32[]{:S(2)}, u32[]{:S(2)}) %collective-permute-start.6) | collective-permute-done | bytes 262176 | tf_op jit(solution)/shard_map/ppermute | solution.py:284
  23.1 1.9 %collective-permute-start.1 = (bf16[2,32,1024]{2,1,0:T(8,128)(2,1)S(1)}, bf16[2,32,1024]{2,1,0:T(8,128)(2,1)S(1)}, u32[]{:S(2)}, u32[]{:S(2)}) collective-permute-start(bf16[2,32,1024]{2,1,0:T(8,128)(2,1)S(1)} %get-tuple-element.26), channel_id=1, source_target_pairs={{0,9},{1,8},{2,11},{3,10},{4,13},{5,12},{6,15},{7,14},{8,1},{9,0},... | collective-permute-start | bytes 393224 | tf_op jit(solution)/shard_map/ppermute | solution.py:284
  24.9 0.0 collective-permute-done.7.refs_3_
  24.9 0.0 collective-permute-start.2
  24.9 2.1 %early.1.refs_2_.refs_3_ = bf16[4,2,64,1024]{3,2,1,0:T(8,128)(2,1)S(1)} custom-call(s32[2,4]{1,0:T(2,128)S(1)} %copy-done.3, s32[2,4]{1,0:T(2,128)S(1)} %collective-permute-done.other, bf16[2,64,1024]{2,1,0:T(8,128)(2,1)S(1)} %collective-permute-done.5.refs_0_, bf16[2,64,1024]{2,1,0:T(8,128)(2,1)S(1)} %collective-permute-done.6.refs_1_, ...), custom_call_target="tpu_custom_call" | custom-call | tf_op jit(solution)/shard_map/early/pallas_call | solution.py:296
  27.1 0.0 copy-start.1
  27.1 0.0 copy-start.2
  27.1 0.0 copy-start.4
  27.1 0.0 collective-permute-done.9.refs_1_
  27.1 0.5 %first_half.1.refs_3_.refs_4_ = f32[6,64,1024]{2,1,0:T(8,128)S(1)} custom-call(bf16[2,64,1024]{2,1,0:T(8,128)(2,1)S(1)} %collective-permute-done.8.refs_0_, bf16[2,64,1024]{2,1,0:T(8,128)(2,1)S(1)} %collective-permute-done.9.refs_1_, bf16[4,2,64,1024]{3,2,1,0:T(8,128)(2,1)S(1)} %early.1.refs_2_.refs_3_), custom_call_target="tpu_custom_call" | custom-call | tf_op jit(solution)/shard_map/first_half/pallas_call | solution.py:305
  27.6 0.0 collective-permute-done.3.refs_0_
  27.7 1.0 %collective-permute-done.4.refs_1_ = bf16[2,32,1024]{2,1,0:T(8,128)(2,1)S(1)} collective-permute-done((bf16[2,32,1024]{2,1,0:T(8,128)(2,1)S(1)}, bf16[2,32,1024]{2,1,0:T(8,128)(2,1)S(1)}, u32[]{:S(2)}, u32[]{:S(2)}) %collective-permute-start.4) | collective-permute-done | bytes 131104 | tf_op jit(solution)/shard_map/ppermute | solution.py:284
  28.7 1.4 %shard_map.66.refs_2_ = bf16[4,4,56,128]{3,2,1,0:T(8,128)(2,1)S(1)} custom-call(s32[3,4]{1,0:T(4,128)S(1)} %copy-done.4, s32[2,4]{1,0:T(2,128)S(1)} %copy-done.3, s32[2,4]{1,0:T(2,128)S(1)} %collective-permute-done.other, bf16[2,32,1024]{2,1,0:T(8,128)(2,1)S(1)} %collective-permute-done.3.refs_0_, bf16[2,32,1024]{2,1,0:T(8,128)(2,1)S(1)} %collective-permute-done.4.refs_1_, ...), custom_call_target="tpu_custom_call" | custom-call | tf_op jit(solution)/shard_map/pallas_call | solution.py:319
  30.1 0.0 collective-permute-done.1.refs_0_
  30.1 1.2 %collective-permute-done.2.refs_1_ = bf16[2,32,1024]{2,1,0:T(8,128)(2,1)S(1)} collective-permute-done((bf16[2,32,1024]{2,1,0:T(8,128)(2,1)S(1)}, bf16[2,32,1024]{2,1,0:T(8,128)(2,1)S(1)}, u32[]{:S(2)}, u32[]{:S(2)}) %collective-permute-start.2) | collective-permute-done | bytes 131104 | tf_op jit(solution)/shard_map/ppermute | solution.py:284
  31.3 1.4 %shard_map.67 = bf16[4,4,56,128]{3,2,1,0:T(8,128)(2,1)S(1)} custom-call(s32[3,4]{1,0:T(4,128)S(1)} %copy-done.4, s32[2,4]{1,0:T(2,128)S(1)} %copy-done.3, s32[2,4]{1,0:T(2,128)S(1)} %collective-permute-done.other, bf16[2,32,1024]{2,1,0:T(8,128)(2,1)S(1)} %collective-permute-done.1.refs_0_, bf16[2,32,1024]{2,1,0:T(8,128)(2,1)S(1)} %collective-permute-done.2.refs_1_, ...), custom_call_target="tpu_custom_call" | custom-call | tf_op jit(solution)/shard_map/pallas_call | solution.py:319
  32.7 16.2 %all_to_all.5 = bf16[16,56,128]{2,1,0:T(8,128)(2,1)S(1)} all-to-all(bf16[16,56,128]{2,1,0:T(8,128)(2,1)S(1)} %bitcast.15), channel_id=1, replica_groups={{0,2,4,6,8,10,12,14,16,18,20,22,24,26,28,30},{1,3,5,7,9,11,13,15,17,19,..., dimensions={0} | all-to-all | bytes 458752 | tf_op jit(solution)/shard_map/all_to_all | solution.py:334
  48.9 0.8 %finish.1 = f32[3,64,129]{2,1,0:T(8,128)} custom-call(bf16[4,4,56,128]{3,2,1,0:T(8,128)(2,1)S(1)} %bitcast.14), custom_call_target="tpu_custom_call" | custom-call | tf_op jit(solution)/shard_map/finish/pallas_call | solution.py:342
  (7 shorter events, 0.0 us)
Async XLA Ops:
  0.0 6.6 %copy-start = (bf16[1024,1024]{1,0:T(8,128)(2,1)S(1)}, bf16[1024,1024]{1,0:T(8,128)(2,1)}, u32[]{:S(2)}) copy-start(bf16[1024,1024]{1,0:T(8,128)(2,1)} %constant.8.refs_6_.refs_4_) | copy-start | bytes 6291460
  0.0 6.6 %copy-start.3 = (s32[2,4]{1,0:T(2,128)S(1)}, s32[2,4]{1,0:T(2,128)}, u32[]{:S(2)}) copy-start(s32[2,4]{1,0:T(2,128)} %valid.7) | copy-start | bytes 100
  1.1 12.5 %collective-permute-start.5 = (bf16[2,64,1024]{2,1,0:T(8,128)(2,1)S(1)}, bf16[2,64,1024]{2,1,0:T(8,128)(2,1)S(1)}, u32[]{:S(2)}, u32[]{:S(2)}) collective-permute-start(bf16[2,64,1024]{2,1,0:T(8,128)(2,1)S(1)} %bitcast.16), channel_id=1, source_target_pairs={{0,24},{1,25},{2,26},{3,27},{4,28},{5,29},{6,30},{7,31},{8,16},{9,... | collective-permute-start | bytes 786440 | tf_op jit(solution)/shard_map/ppermute | solution.py:284
  8.7 9.2 %collective-permute-start.8 = (bf16[2,64,1024]{2,1,0:T(8,128)(2,1)S(1)}, bf16[2,64,1024]{2,1,0:T(8,128)(2,1)S(1)}, u32[]{:S(2)}, u32[]{:S(2)}) collective-permute-start(bf16[2,64,1024]{2,1,0:T(8,128)(2,1)S(1)} %get-tuple-element.33), channel_id=1, source_target_pairs={{0,8},{1,9},{2,10},{3,11},{4,12},{5,13},{6,14},{7,15},{8,0},{9,1},... | collective-permute-start | bytes 786440 | tf_op jit(solution)/shard_map/ppermute | solution.py:284
  9.3 13.7 %collective-permute-start.6 = (bf16[2,64,1024]{2,1,0:T(8,128)(2,1)S(1)}, bf16[2,64,1024]{2,1,0:T(8,128)(2,1)S(1)}, u32[]{:S(2)}, u32[]{:S(2)}) collective-permute-start(bf16[2,64,1024]{2,1,0:T(8,128)(2,1)S(1)} %bitcast.25), channel_id=1, source_target_pairs={{0,25},{1,24},{2,27},{3,26},{4,29},{5,28},{6,31},{7,30},{8,17},{9,... | collective-permute-start | bytes 786440 | tf_op jit(solution)/shard_map/ppermute | solution.py:284
  9.7 15.3 %collective-permute-start.7 = (bf16[2,64,1024]{2,1,0:T(8,128)(2,1)S(1)}, bf16[2,64,1024]{2,1,0:T(8,128)(2,1)S(1)}, u32[]{:S(2)}, u32[]{:S(2)}) collective-permute-start(bf16[2,64,1024]{2,1,0:T(8,128)(2,1)S(1)} %bitcast.24), channel_id=1, source_target_pairs={{0,1},{1,0},{2,3},{3,2},{4,5},{5,4},{6,7},{7,6},{8,9},{9,8},{10,11... | collective-permute-start | bytes 786440 | tf_op jit(solution)/shard_map/ppermute | solution.py:284
  10.9 1.2 %collective-permute-start = (s32[2,4]{1,0:T(2,128)S(1)}, s32[2,4]{1,0:T(2,128)S(1)}, u32[]{:S(2)}, u32[]{:S(2)}) collective-permute-start(s32[2,4]{1,0:T(2,128)S(1)} %copy-done.3), channel_id=1, source_target_pairs={{0,1},{1,0},{2,3},{3,2},{4,5},{5,4},{6,7},{7,6},{8,9},{9,8},{10,11... | collective-permute-start | bytes 104 | tf_op jit(solution)/shard_map/ppermute | solution.py:290
  12.1 15.0 %collective-permute-start.9 = (bf16[2,64,1024]{2,1,0:T(8,128)(2,1)S(1)}, bf16[2,64,1024]{2,1,0:T(8,128)(2,1)S(1)}, u32[]{:S(2)}, u32[]{:S(2)}) collective-permute-start(bf16[2,64,1024]{2,1,0:T(8,128)(2,1)S(1)} %get-tuple-element.34), channel_id=1, source_target_pairs={{0,16},{1,17},{2,18},{3,19},{4,20},{5,21},{6,22},{7,23},{8,24},{9,... | collective-permute-start | bytes 786440 | tf_op jit(solution)/shard_map/ppermute | solution.py:284
  13.6 14.1 %collective-permute-start.3 = (bf16[2,32,1024]{2,1,0:T(8,128)(2,1)S(1)}, bf16[2,32,1024]{2,1,0:T(8,128)(2,1)S(1)}, u32[]{:S(2)}, u32[]{:S(2)}) collective-permute-start(bf16[2,32,1024]{2,1,0:T(8,128)(2,1)S(1)} %get-tuple-element.28), channel_id=1, source_target_pairs={{0,9},{1,8},{2,11},{3,10},{4,13},{5,12},{6,15},{7,14},{8,1},{9,0},... | collective-permute-start | bytes 393224 | tf_op jit(solution)/shard_map/ppermute | solution.py:284
  18.0 10.7 %collective-permute-start.4 = (bf16[2,32,1024]{2,1,0:T(8,128)(2,1)S(1)}, bf16[2,32,1024]{2,1,0:T(8,128)(2,1)S(1)}, u32[]{:S(2)}, u32[]{:S(2)}) collective-permute-start(bf16[2,32,1024]{2,1,0:T(8,128)(2,1)S(1)} %get-tuple-element.29), channel_id=1, source_target_pairs={{0,17},{1,16},{2,19},{3,18},{4,21},{5,20},{6,23},{7,22},{8,25},{9,... | collective-permute-start | bytes 393224 | tf_op jit(solution)/shard_map/ppermute | solution.py:284
  23.1 7.0 %collective-permute-start.1 = (bf16[2,32,1024]{2,1,0:T(8,128)(2,1)S(1)}, bf16[2,32,1024]{2,1,0:T(8,128)(2,1)S(1)}, u32[]{:S(2)}, u32[]{:S(2)}) collective-permute-start(bf16[2,32,1024]{2,1,0:T(8,128)(2,1)S(1)} %get-tuple-element.26), channel_id=1, source_target_pairs={{0,9},{1,8},{2,11},{3,10},{4,13},{5,12},{6,15},{7,14},{8,1},{9,0},... | collective-permute-start | bytes 393224 | tf_op jit(solution)/shard_map/ppermute | solution.py:284
  24.9 6.3 %collective-permute-start.2 = (bf16[2,32,1024]{2,1,0:T(8,128)(2,1)S(1)}, bf16[2,32,1024]{2,1,0:T(8,128)(2,1)S(1)}, u32[]{:S(2)}, u32[]{:S(2)}) collective-permute-start(bf16[2,32,1024]{2,1,0:T(8,128)(2,1)S(1)} %get-tuple-element.27), channel_id=1, source_target_pairs={{0,17},{1,16},{2,19},{3,18},{4,21},{5,20},{6,23},{7,22},{8,25},{9,... | collective-permute-start | bytes 393224 | tf_op jit(solution)/shard_map/ppermute | solution.py:284
  27.1 1.7 %copy-start.1 = (bf16[1024,256]{1,0:T(8,128)(2,1)S(1)}, bf16[1024,256]{1,0:T(8,128)(2,1)}, u32[]{:S(2)}) copy-start(bf16[1024,256]{1,0:T(8,128)(2,1)} %constant.12.refs_5_.refs_6_) | copy-start | bytes 1572868
  27.1 1.6 %copy-start.2 = (bf16[1024,256]{1,0:T(8,128)(2,1)S(1)}, bf16[1024,256]{1,0:T(8,128)(2,1)}, u32[]{:S(2)}) copy-start(bf16[1024,256]{1,0:T(8,128)(2,1)} %constant.9.refs_4_.refs_5_) | copy-start | bytes 1572868
  27.1 1.6 %copy-start.4 = (s32[3,4]{1,0:T(4,128)S(1)}, s32[3,4]{1,0:T(4,128)}, u32[]{:S(2)}) copy-start(s32[3,4]{1,0:T(4,128)} %plan.3) | copy-start | bytes 148

commit v2 on v1

--- a/solution.py
+++ b/solution.py
@@ -13,7 +13,7 @@
 LAGS = 129
 LANES = 128
 STEP = 16
-PARTS = 2
+PARTS = 4
 
 
 def dft_table(length, count):
@@ -67,13 +67,26 @@
     whiten([(piece, out, lambda window: valid[window, here]) for piece, out in zip(pieces, outs, strict=True)], table, spec)
 
 
-def early_kernel(slots, valid, other, *refs):
-    pieces, (table, out, spec) = refs[:-3], refs[-3:]
+def early_kernel(slots, plan, valid, other, *refs):
+    pieces, (table, out, tails, order, spec) = refs[:-5], refs[-5:]
     here = lax.axis_index("chan")
+    rounds, blocks = plan.shape
+    tails[...] = jnp.zeros_like(tails)
+    for block in range(blocks):
+        for step in range(1, blocks):
+            count = 0
+            for mask in (valid, other):
+                for window in range(mask.shape[0]):
+                    count = count + mask[window, block] * mask[window, block ^ step]
+            tails[block, rounds + step - 1 : rounds + step, :] = jnp.full((1, LANES), count.astype(jnp.float32))
+    for turn in range(rounds):
+        for step in range(1, blocks):
+            met = (plan[turn, here] == here ^ step).astype(jnp.float32)
+            order[turn, step - 1 : step, :] = jnp.full((1, LANES), met)
     listed = []
-    for order, ((half, slot), piece) in enumerate(zip(slots, pieces, strict=True)):
+    for number, ((half, slot), piece) in enumerate(zip(slots, pieces, strict=True)):
         mask = (valid, other)[half]
-        listed.append((piece, out.at[order], lambda window, mask=mask, slot=slot: mask[window, here ^ slot]))
+        listed.append((piece, out.at[number], lambda window, mask=mask, slot=slot: mask[window, here ^ slot]))
     whiten(listed, table, spec)
 
 
@@ -122,10 +135,10 @@
                 stack[pair, row : row + STEP, bins + lane : bins + lane + LANES] = sums[1]
 
 
-def second_kernel(rounds, early_slots, late, part, plan, valid, other, *refs):
+def second_kernel(rounds, early_slots, late, part, *refs):
     head, refs = refs[: len(late)], refs[len(late) :]
     done, refs = refs[:part], refs[part:]
-    early, stack, lag_hi, lag_lo, out, both, main, extra = refs
+    early, stack, tails, lag_hi, lag_lo, out, both, main, extra = refs
     here = lax.axis_index("chan")
     windows, rows, width = head[0].shape
     base = part * rows
@@ -151,7 +164,7 @@
     dot = functools.partial(jnp.dot, preferred_element_type=jnp.float32)
     double = dot(both[...], lag_hi[...])
     main[...] = double[:height] + double[height:] + dot(both[:height, :], lag_lo[...])
-    extra[...] = jnp.zeros_like(extra)
+    extra[...] = tails[...]
     group = (out.shape[2] - 8) // rounds
     zones = rows // group
     for earlier, ref in enumerate(done):
@@ -160,23 +173,14 @@
     diagonal = lax.broadcasted_iota(jnp.int32, (rows, LANES), 0) == lax.broadcasted_iota(jnp.int32, (rows, LANES), 1)
     for pair, slots in enumerate(pairs):
         blocks = [slot ^ here for slot in slots]
-        step = 0
-        for turn in range(1, rounds):
-            step = step + turn * (plan[turn, blocks[0]] == blocks[1]).astype(jnp.int32)
-        count = 0
-        for mask in (valid, other):
-            for window in range(mask.shape[0]):
-                count = count + mask[window, blocks[0]] * mask[window, blocks[1]]
-        count = jnp.full((1, LANES), count.astype(jnp.float32))
-        place = pl.ds(pl.multiple_of(step * group, group), group)
+        step = (slots[0] ^ slots[1]) - 1
         for side in range(2):
             value = main[pair * rows : (pair + 1) * rows, side * LANES : (side + 1) * LANES]
             value = value.astype(jnp.bfloat16).reshape(zones, group, LANES)
-            out[blocks[side], first_zone : first_zone + zones, place, :] = value
+            out[blocks[side], first_zone : first_zone + zones, step * group : (step + 1) * group, :] = value
             mirror = main[pair * rows : (pair + 1) * rows, (1 - side) * LANES : (1 - side) * LANES + 1]
             end = jnp.sum(jnp.where(diagonal, mirror, 0.0), axis=0, keepdims=True)
-            extra[blocks[side], pl.ds(step, 1), :] = end
-            extra[blocks[side], pl.ds(rounds + step, 1), :] = count
+            extra[blocks[side], step : step + 1, :] = end
     for block in range(out.shape[0]):
         tail = extra[block].astype(jnp.bfloat16)
         for zone in range(zones):
@@ -196,7 +200,7 @@
         copy.wait()
 
 
-def last_kernel(rounds, per_part, parts, out):
+def last_kernel(rounds, per_part, parts, order, out):
     blocks, zones, _, _ = parts.shape
     group = out.shape[1] // blocks
     lane = lax.broadcasted_iota(jnp.int32, (group, LANES), 1)
@@ -210,12 +214,21 @@
         tail = total[rounds * group : rounds * group + 8]
         if inverse is None:
             inverse = 1.0 / tail[rounds : 2 * rounds]
+        values, ends = [], []
         for step in range(rounds):
             scale = inverse[step : step + 1]
-            rows = slice(block * group, (block + 1) * group)
-            out[step, rows, :LANES] = total[step * group : (step + 1) * group] * scale
+            values.append(total[step * group : (step + 1) * group] * scale)
             end = jnp.where(chosen, tail[step : step + 1] * scale, 0.0)
-            out[step, rows, LANES:] = jnp.sum(end, axis=1, keepdims=True)
+            ends.append(jnp.sum(end, axis=1, keepdims=True))
+        rows = slice(block * group, (block + 1) * group)
+        for turn in range(rounds):
+            value, end = values[0], ends[0]
+            for step in range(1, rounds):
+                met = order[turn, step : step + 1, :] > 0.5
+                value = jnp.where(met, values[step], value)
+                end = jnp.where(met[:, :1], ends[step], end)
+            out[turn, rows, :LANES] = value
+            out[turn, rows, LANES:] = end
 
 
 def by_channels(samples, valid, plan):
@@ -293,15 +306,19 @@
     lags = np.concatenate([lag_table(bins, length, shifts, s) for s in (1.0, -1.0)], axis=1)
     lag_hi, lag_lo = high_low(lags)
 
-    early = pl.pallas_call(
+    early, tails, order = pl.pallas_call(
         functools.partial(early_kernel, early_slots),
-        out_shape=jax.ShapeDtypeStruct((len(early_slots), windows, rows, length), jnp.bfloat16),
-        in_specs=[smem] * 2 + [vmem] * (len(early_slots) + 1),
-        out_specs=vmem,
+        out_shape=[
+            jax.ShapeDtypeStruct((len(early_slots), windows, rows, length), jnp.bfloat16),
+            jax.ShapeDtypeStruct((chan_count, 8, LANES), jnp.float32),
+            jax.ShapeDtypeStruct((rounds, 8, LANES), jnp.float32),
+        ],
+        in_specs=[smem] * 3 + [vmem] * (len(early_slots) + 1),
+        out_specs=[vmem] * 3,
         scratch_shapes=[pltpu.VMEM((len(early_slots) * windows * rows, length), jnp.float32)],
         compiler_params=params,
         name="early",
-    )(valid, other, *early_pieces, table)
+    )(plan, valid, other, *early_pieces, table)
     stack = pl.pallas_call(
         functools.partial(first_kernel, early_slots, late_steps),
         out_shape=jax.ShapeDtypeStruct((pairs, rows, length), jnp.float32),
@@ -319,7 +336,7 @@
             pl.pallas_call(
                 functools.partial(second_kernel, rounds, early_slots, late_steps, part),
                 out_shape=jax.ShapeDtypeStruct((chan_count, zones, height, LANES), jnp.bfloat16),
-                in_specs=[smem] * 3 + [vmem] * (len(late_steps) + part + 4),
+                in_specs=[vmem] * (len(late_steps) + part + 5),
                 out_specs=vmem,
                 scratch_shapes=[
                     pltpu.VMEM((2 * pairs * part_rows, length), jnp.bfloat16),
@@ -327,7 +344,7 @@
                     pltpu.VMEM((chan_count, 8, LANES), jnp.float32),
                 ],
                 compiler_params=params,
-            )(plan, valid, other, *heads, *sent, early, stack, lag_hi, lag_lo)
+            )(*heads, *sent, early, stack, tails, lag_hi, lag_lo)
         )
     sent = sent[-1]
     same_half = [[a * time_count + z * 2 + c for a in range(chan_count) for z in range(zones)] for c in range(2)]
@@ -342,11 +359,11 @@
     result = pl.pallas_call(
         functools.partial(last_kernel, rounds, per_part),
         out_shape=jax.ShapeDtypeStruct((rounds, chan_count * group, LAGS), jnp.float32),
-        in_specs=[vmem],
+        in_specs=[vmem] * 2,
         out_specs=vmem,
         compiler_params=params,
         name="finish",
-    )(parts)
+    )(parts, order)
     return result.transpose(1, 0, 2)
 
 

time: 49.9 us -> 55.3 us (1.11)
  starting transfers between devices: 9.75 us -> 13.6 us
  blocking collectives: 16.2 us -> 17.4 us
  local copies, waits for them, and re-layouts: 0.03 us -> 1.15 us
  Pallas kernels: 11 us -> 10.1 us
    ppermute x9 -> x13, starting transfers between devices: 9.74 us -> 13.1 us  [by_channels(): piece = lax.ppermute(piece, ('chan', 'tm'), partners(*key))]
    all_to_all x1, blocking collectives: 16.2 us -> 17.4 us  [by_channels(): lax.all_to_all(sent.reshape(chan_count * zones, height, LANES), ('chan',...]
    ppermute x1, waiting for transfers between devices: 1.16 us -> 0.01 us  [by_channels(): other = lax.ppermute(valid, ('chan', 'tm'), partners(1, 0))]
    ppermute x9 -> x13, waiting for transfers between devices: 11.5 us -> 12.6 us  [by_channels(): piece = lax.ppermute(piece, ('chan', 'tm'), partners(*key))]
    unnamed x10, local copies, waits for them, and re-layouts: 0.03 us -> 1.15 us
    pallas_call x2 -> x4, Pallas kernels: 2.8 us -> 2 us  [by_channels(): pl.pallas_call(functools.partial(second_kernel, rounds, early_slots, late...]
    ppermute x1, starting transfers between devices: 0.01 us -> 0.57 us  [by_channels(): other = lax.ppermute(valid, ('chan', 'tm'), partners(1, 0))]
  transfers between devices with their start and end apart: 10 -> 14, of which waited for: 5 -> 4; matrix products, arithmetic and copies ran while one was open for 0% -> 0% of each run, Pallas kernels for 15% -> 9%
where the time goes in v2:
time: 55.3 us; the launch traced here: 55.1 us
  blocking collectives  17.4 us (31%)
  starting transfers between devices  13.6 us (25%)
  waiting for transfers between devices  12.6 us (23%)
  Pallas kernels  10.1 us (18%)
  local copies, waits for them, and re-layouts  1.15 us (2%)
    all_to_all x1, blocking collectives, by_channels(): lax.all_to_all(sent.reshape(chan_count * zones, height, LANES), ('chan',...  17.4 us
    ppermute x13, starting transfers between devices, by_channels(): piece = lax.ppermute(piece, ('chan', 'tm'), partners(*key))  13.1 us
    ppermute x13, waiting for transfers between devices, by_channels(): piece = lax.ppermute(piece, ('chan', 'tm'), partners(*key))  12.6 us
    pallas_call x2, Pallas kernels, cut(): pl.pallas_call(functools.partial(cut_kernel, keys, zone_ranges), out_shap...  2.6 us
    pallas_call x1, Pallas kernels, by_channels(): pl.pallas_call(functools.partial(early_kernel, early_slots), out_shape=[j...  2.13 us
    pallas_call x1, Pallas kernels, by_channels(): pl.pallas_call(functools.partial(sent_kernel, len(late_raw)), out_shape=[...  2.08 us
    pallas_call x4, Pallas kernels, by_channels(): pl.pallas_call(functools.partial(second_kernel, rounds, early_slots, late...  2 us
    unnamed x10, local copies, waits for them, and re-layouts  1.15 us
  transfers between devices with their start and end apart: 14, of which 4 were waited for; matrix products, arithmetic and copies ran while one was open for 0% of the time, Pallas kernels for 9%

profile of v2, /device:TPU:0, one launch (start us, length us, event | category | flops | bytes accessed | tf_op | source)
XLA Modules:
  0.0 55.1 jit_solution(7532173332537115735)
XLA Ops:
  0.0 1.6 %shard_map.64 = (bf16[2,4,16,1024]{3,2,1,0:T(8,128)(2,1)S(1)}, bf16[2,4,16,1024]{3,2,1,0:T(8,128)(2,1)S(1)}, bf16[2,4,16,1024]{3,2,1,0:T(8,128)(2,1)S(1)}, bf16[...) custom-call(bf16[2,4,2,4,16,1024]{5,4,3,2,1,0:T(8,128)(2,1)} %bitcast.34), custom_call_target="tpu_custom_call" | custom-call | tf_op jit(solution)/shard_map/pallas_call | solution.py:250
  1.7 0.5 copy-done
  2.2 2.1 %whiten_sent.1 = (bf16[2,64,1024]{2,1,0:T(8,128)(2,1)S(1)}, bf16[2,64,1024]{2,1,0:T(8,128)(2,1)S(1)}, bf16[2,16,1024]{2,1,0:T(8,128)(2,1)S(1)}, bf16[2,16,1024]{...) custom-call(s32[2,4]{1,0:T(2,128)S(1)} %copy-done.3, ...), custom_call_target="tpu_custom_call" | custom-call | tf_op jit(solution)/shard_map/whiten_sent/pallas_call | solution.py:285
  4.2 2.5 %collective-permute-start.2 = (bf16[2,16,1024]{2,1,0:T(8,128)(2,1)S(1)}, bf16[2,16,1024]{2,1,0:T(8,128)(2,1)S(1)}, u32[]{:S(2)}, u32[]{:S(2)}) collective-permute-start(bf16[2,16,1024]{2,1,0:T(8,128)(2,1)S(1)} %get-tuple-element.43), channel_id=1, source_target_pairs={{0,9},{1,8},{2,11},{3,10},{4,13},{5,12},{6,15},{7,14},{8,1},{9,0},... | collective-permute-start | bytes 196616 | tf_op jit(solution)/shard_map/ppermute | solution.py:297
  6.7 1.8 %collective-permute-start.3 = (bf16[2,16,1024]{2,1,0:T(8,128)(2,1)S(1)}, bf16[2,16,1024]{2,1,0:T(8,128)(2,1)S(1)}, u32[]{:S(2)}, u32[]{:S(2)}) collective-permute-start(bf16[2,16,1024]{2,1,0:T(8,128)(2,1)S(1)} %get-tuple-element.44), channel_id=1, source_target_pairs={{0,17},{1,16},{2,19},{3,18},{4,21},{5,20},{6,23},{7,22},{8,25},{9,... | collective-permute-start | bytes 196616 | tf_op jit(solution)/shard_map/ppermute | solution.py:297
  8.5 0.1 collective-permute-start.10
  8.6 0.6 %collective-permute-start.4 = (s32[2,4]{1,0:T(2,128)S(1)}, s32[2,4]{1,0:T(2,128)S(1)}, u32[]{:S(2)}, u32[]{:S(2)}) collective-permute-start(s32[2,4]{1,0:T(2,128)S(1)} %copy-done.3), channel_id=1, source_target_pairs={{0,1},{1,0},{2,3},{3,2},{4,5},{5,4},{6,7},{7,6},{8,9},{9,8},{10,11... | collective-permute-start | bytes 104 | tf_op jit(solution)/shard_map/ppermute | solution.py:303
  9.2 1.0 %shard_map.65 = bf16[2,4,16,1024]{3,2,1,0:T(8,128)(2,1)S(1)} custom-call(bf16[2,4,2,4,16,1024]{5,4,3,2,1,0:T(8,128)(2,1)} %bitcast.35), custom_call_target="tpu_custom_call" | custom-call | tf_op jit(solution)/shard_map/pallas_call | solution.py:250
  10.1 1.5 %collective-permute-start.5 = (bf16[2,64,1024]{2,1,0:T(8,128)(2,1)S(1)}, bf16[2,64,1024]{2,1,0:T(8,128)(2,1)S(1)}, u32[]{:S(2)}, u32[]{:S(2)}) collective-permute-start(bf16[2,64,1024]{2,1,0:T(8,128)(2,1)S(1)} %bitcast.21), channel_id=1, source_target_pairs={{0,24},{1,25},{2,26},{3,27},{4,28},{5,29},{6,30},{7,31},{8,16},{9,... | collective-permute-start | bytes 786440 | tf_op jit(solution)/shard_map/ppermute | solution.py:297
  11.6 0.1 collective-permute-start.8
  11.8 1.9 %collective-permute-start.9 = (bf16[2,64,1024]{2,1,0:T(8,128)(2,1)S(1)}, bf16[2,64,1024]{2,1,0:T(8,128)(2,1)S(1)}, u32[]{:S(2)}, u32[]{:S(2)}) collective-permute-start(bf16[2,64,1024]{2,1,0:T(8,128)(2,1)S(1)} %get-tuple-element.50), channel_id=1, source_target_pairs={{0,16},{1,17},{2,18},{3,19},{4,20},{5,21},{6,22},{7,23},{8,24},{9,... | collective-permute-start | bytes 786440 | tf_op jit(solution)/shard_map/ppermute | solution.py:297
  13.7 0.2 collective-permute-start.6
  13.9 1.3 %collective-permute-start.7 = (bf16[2,64,1024]{2,1,0:T(8,128)(2,1)S(1)}, bf16[2,64,1024]{2,1,0:T(8,128)(2,1)S(1)}, u32[]{:S(2)}, u32[]{:S(2)}) collective-permute-start(bf16[2,64,1024]{2,1,0:T(8,128)(2,1)S(1)} %bitcast.32), channel_id=1, source_target_pairs={{0,1},{1,0},{2,3},{3,2},{4,5},{5,4},{6,7},{7,6},{8,9},{9,8},{10,11... | collective-permute-start | bytes 786440 | tf_op jit(solution)/shard_map/ppermute | solution.py:297
  15.3 5.1 %collective-permute-done.5.refs_0_ = bf16[2,64,1024]{2,1,0:T(8,128)(2,1)S(1)} collective-permute-done((bf16[2,64,1024]{2,1,0:T(8,128)(2,1)S(1)}, bf16[2,64,1024]{2,1,0:T(8,128)(2,1)S(1)}, u32[]{:S(2)}, u32[]{:S(2)}) %collective-permute-start.5) | collective-permute-done | bytes 262176 | tf_op jit(solution)/shard_map/ppermute | solution.py:297
  20.3 4.2 %collective-permute-done.8.refs_0_ = bf16[2,64,1024]{2,1,0:T(8,128)(2,1)S(1)} collective-permute-done((bf16[2,64,1024]{2,1,0:T(8,128)(2,1)S(1)}, bf16[2,64,1024]{2,1,0:T(8,128)(2,1)S(1)}, u32[]{:S(2)}, u32[]{:S(2)}) %collective-permute-start.8) | collective-permute-done | bytes 262176 | tf_op jit(solution)/shard_map/ppermute | solution.py:297
  24.5 1.3 %collective-permute-done.9.refs_1_ = bf16[2,64,1024]{2,1,0:T(8,128)(2,1)S(1)} collective-permute-done((bf16[2,64,1024]{2,1,0:T(8,128)(2,1)S(1)}, bf16[2,64,1024]{2,1,0:T(8,128)(2,1)S(1)}, u32[]{:S(2)}, u32[]{:S(2)}) %collective-permute-start.9) | collective-permute-done | bytes 262176 | tf_op jit(solution)/shard_map/ppermute | solution.py:297
  25.9 1.9 %collective-permute-start.12 = (bf16[2,16,1024]{2,1,0:T(8,128)(2,1)S(1)}, bf16[2,16,1024]{2,1,0:T(8,128)(2,1)S(1)}, u32[]{:S(2)}, u32[]{:S(2)}) collective-permute-start(bf16[2,16,1024]{2,1,0:T(8,128)(2,1)S(1)} %get-tuple-element.54), channel_id=1, source_target_pairs={{0,9},{1,8},{2,11},{3,10},{4,13},{5,12},{6,15},{7,14},{8,1},{9,0},... | collective-permute-start | bytes 196616 | tf_op jit(solution)/shard_map/ppermute | solution.py:297
  27.7 2.0 %collective-permute-done.6.refs_1_ = bf16[2,64,1024]{2,1,0:T(8,128)(2,1)S(1)} collective-permute-done((bf16[2,64,1024]{2,1,0:T(8,128)(2,1)S(1)}, bf16[2,64,1024]{2,1,0:T(8,128)(2,1)S(1)}, u32[]{:S(2)}, u32[]{:S(2)}) %collective-permute-start.6) | collective-permute-done | bytes 262176 | tf_op jit(solution)/shard_map/ppermute | solution.py:297
  29.7 1.3 %collective-permute-start.13 = (bf16[2,16,1024]{2,1,0:T(8,128)(2,1)S(1)}, bf16[2,16,1024]{2,1,0:T(8,128)(2,1)S(1)}, u32[]{:S(2)}, u32[]{:S(2)}) collective-permute-start(bf16[2,16,1024]{2,1,0:T(8,128)(2,1)S(1)} %get-tuple-element.55), channel_id=1, source_target_pairs={{0,17},{1,16},{2,19},{3,18},{4,21},{5,20},{6,23},{7,22},{8,25},{9,... | collective-permute-start | bytes 196616 | tf_op jit(solution)/shard_map/ppermute | solution.py:297
  31.1 0.4 collective-permute-start.1
  31.5 2.1 %early.1 = (bf16[4,2,64,1024]{3,2,1,0:T(8,128)(2,1)S(1)}, f32[4,8,128]{2,1,0:T(8,128)S(1)}, f32[3,8,128]{2,1,0:T(8,128)S(1)}) custom-call(s32[3,4]{1,0:T(4,128)S(1)} %copy-done.4, s32[2,4]{1,0:T(2,128)S(1)} %copy-done.3, s32[2,4]{1,0:T(2,128)S(1)} %collective-permute-done.4.other, bf16[2,64,1024]{2,1,0:T(8,128)(2,1)S(1)} %collective-permute-done.5.refs_0_, ...), custom_call_target="tpu_custom_call" | custom-call | tf_op jit(solution)/shard_map/early/pallas_call | solution.py:309
  33.6 0.0 copy-start.1
  33.6 0.0 copy-start.2
  33.6 0.5 first_half.1.refs_3_.refs_4_.refs_5_.refs_6_
  34.2 0.5 copy-done.1
  34.7 0.2 copy-done.2
  34.8 0.5 shard_map.66.refs_2_
  35.3 0.5 shard_map.67.refs_3_
  35.9 0.5 shard_map.68.refs_4_
  36.4 0.5 shard_map.69
  36.9 17.4 %all_to_all.5 = bf16[16,56,128]{2,1,0:T(8,128)(2,1)S(1)} all-to-all(bf16[16,56,128]{2,1,0:T(8,128)(2,1)S(1)} %bitcast.19), channel_id=1, replica_groups={{0,2,4,6,8,10,12,14,16,18,20,22,24,26,28,30},{1,3,5,7,9,11,13,15,17,19,..., dimensions={0} | all-to-all | bytes 458752 | tf_op jit(solution)/shard_map/all_to_all | solution.py:351
  54.3 0.8 %finish.1 = f32[3,64,129]{2,1,0:T(8,128)} custom-call(bf16[4,4,56,128]{3,2,1,0:T(8,128)(2,1)S(1)} %bitcast.18, f32[3,8,128]{2,1,0:T(8,128)S(1)} %get-tuple-element.56.order), custom_call_target="tpu_custom_call" | custom-call | tf_op jit(solution)/shard_map/finish/pallas_call | solution.py:359
  (17 shorter events, 0.0 us)
Async XLA Ops:
  0.0 2.1 %copy-start = (bf16[1024,1024]{1,0:T(8,128)(2,1)S(1)}, bf16[1024,1024]{1,0:T(8,128)(2,1)}, u32[]{:S(2)}) copy-start(bf16[1024,1024]{1,0:T(8,128)(2,1)} %constant.8.refs_10_.refs_4_) | copy-start | bytes 6291460
  0.0 2.1 %copy-start.3 = (s32[2,4]{1,0:T(2,128)S(1)}, s32[2,4]{1,0:T(2,128)}, u32[]{:S(2)}) copy-start(s32[2,4]{1,0:T(2,128)} %valid.3) | copy-start | bytes 100
  2.1 29.3 %copy-start.4 = (s32[3,4]{1,0:T(4,128)S(1)}, s32[3,4]{1,0:T(4,128)}, u32[]{:S(2)}) copy-start(s32[3,4]{1,0:T(4,128)} %plan.1) | copy-start | bytes 148
  4.2 7.5 %collective-permute-start.2 = (bf16[2,16,1024]{2,1,0:T(8,128)(2,1)S(1)}, bf16[2,16,1024]{2,1,0:T(8,128)(2,1)S(1)}, u32[]{:S(2)}, u32[]{:S(2)}) collective-permute-start(bf16[2,16,1024]{2,1,0:T(8,128)(2,1)S(1)} %get-tuple-element.43), channel_id=1, source_target_pairs={{0,9},{1,8},{2,11},{3,10},{4,13},{5,12},{6,15},{7,14},{8,1},{9,0},... | collective-permute-start | bytes 196616 | tf_op jit(solution)/shard_map/ppermute | solution.py:297
  6.7 7.0 %collective-permute-start.3 = (bf16[2,16,1024]{2,1,0:T(8,128)(2,1)S(1)}, bf16[2,16,1024]{2,1,0:T(8,128)(2,1)S(1)}, u32[]{:S(2)}, u32[]{:S(2)}) collective-permute-start(bf16[2,16,1024]{2,1,0:T(8,128)(2,1)S(1)} %get-tuple-element.44), channel_id=1, source_target_pairs={{0,17},{1,16},{2,19},{3,18},{4,21},{5,20},{6,23},{7,22},{8,25},{9,... | collective-permute-start | bytes 196616 | tf_op jit(solution)/shard_map/ppermute | solution.py:297
  8.5 5.4 %collective-permute-start.10 = (bf16[2,16,1024]{2,1,0:T(8,128)(2,1)S(1)}, bf16[2,16,1024]{2,1,0:T(8,128)(2,1)S(1)}, u32[]{:S(2)}, u32[]{:S(2)}) collective-permute-start(bf16[2,16,1024]{2,1,0:T(8,128)(2,1)S(1)} %get-tuple-element.52), channel_id=1, source_target_pairs={{0,9},{1,8},{2,11},{3,10},{4,13},{5,12},{6,15},{7,14},{8,1},{9,0},... | collective-permute-start | bytes 196616 | tf_op jit(solution)/shard_map/ppermute | solution.py:297
  8.6 3.0 %collective-permute-start.4 = (s32[2,4]{1,0:T(2,128)S(1)}, s32[2,4]{1,0:T(2,128)S(1)}, u32[]{:S(2)}, u32[]{:S(2)}) collective-permute-start(s32[2,4]{1,0:T(2,128)S(1)} %copy-done.3), channel_id=1, source_target_pairs={{0,1},{1,0},{2,3},{3,2},{4,5},{5,4},{6,7},{7,6},{8,9},{9,8},{10,11... | collective-permute-start | bytes 104 | tf_op jit(solution)/shard_map/ppermute | solution.py:303
  10.1 10.2 %collective-permute-start.5 = (bf16[2,64,1024]{2,1,0:T(8,128)(2,1)S(1)}, bf16[2,64,1024]{2,1,0:T(8,128)(2,1)S(1)}, u32[]{:S(2)}, u32[]{:S(2)}) collective-permute-start(bf16[2,64,1024]{2,1,0:T(8,128)(2,1)S(1)} %bitcast.21), channel_id=1, source_target_pairs={{0,24},{1,25},{2,26},{3,27},{4,28},{5,29},{6,30},{7,31},{8,16},{9,... | collective-permute-start | bytes 786440 | tf_op jit(solution)/shard_map/ppermute | solution.py:297
  11.6 12.9 %collective-permute-start.8 = (bf16[2,64,1024]{2,1,0:T(8,128)(2,1)S(1)}, bf16[2,64,1024]{2,1,0:T(8,128)(2,1)S(1)}, u32[]{:S(2)}, u32[]{:S(2)}) collective-permute-start(bf16[2,64,1024]{2,1,0:T(8,128)(2,1)S(1)} %get-tuple-element.49), channel_id=1, source_target_pairs={{0,8},{1,9},{2,10},{3,11},{4,12},{5,13},{6,14},{7,15},{8,0},{9,1},... | collective-permute-start | bytes 786440 | tf_op jit(solution)/shard_map/ppermute | solution.py:297
  11.8 14.1 %collective-permute-start.9 = (bf16[2,64,1024]{2,1,0:T(8,128)(2,1)S(1)}, bf16[2,64,1024]{2,1,0:T(8,128)(2,1)S(1)}, u32[]{:S(2)}, u32[]{:S(2)}) collective-permute-start(bf16[2,64,1024]{2,1,0:T(8,128)(2,1)S(1)} %get-tuple-element.50), channel_id=1, source_target_pairs={{0,16},{1,17},{2,18},{3,19},{4,20},{5,21},{6,22},{7,23},{8,24},{9,... | collective-permute-start | bytes 786440 | tf_op jit(solution)/shard_map/ppermute | solution.py:297
  13.7 16.0 %collective-permute-start.6 = (bf16[2,64,1024]{2,1,0:T(8,128)(2,1)S(1)}, bf16[2,64,1024]{2,1,0:T(8,128)(2,1)S(1)}, u32[]{:S(2)}, u32[]{:S(2)}) collective-permute-start(bf16[2,64,1024]{2,1,0:T(8,128)(2,1)S(1)} %bitcast.33), channel_id=1, source_target_pairs={{0,25},{1,24},{2,27},{3,26},{4,29},{5,28},{6,31},{7,30},{8,17},{9,... | collective-permute-start | bytes 786440 | tf_op jit(solution)/shard_map/ppermute | solution.py:297
  13.9 17.2 %collective-permute-start.7 = (bf16[2,64,1024]{2,1,0:T(8,128)(2,1)S(1)}, bf16[2,64,1024]{2,1,0:T(8,128)(2,1)S(1)}, u32[]{:S(2)}, u32[]{:S(2)}) collective-permute-start(bf16[2,64,1024]{2,1,0:T(8,128)(2,1)S(1)} %bitcast.32), channel_id=1, source_target_pairs={{0,1},{1,0},{2,3},{3,2},{4,5},{5,4},{6,7},{7,6},{8,9},{9,8},{10,11... | collective-permute-start | bytes 786440 | tf_op jit(solution)/shard_map/ppermute | solution.py:297
  20.3 16.0 %collective-permute-start = (bf16[2,16,1024]{2,1,0:T(8,128)(2,1)S(1)}, bf16[2,16,1024]{2,1,0:T(8,128)(2,1)S(1)}, u32[]{:S(2)}, u32[]{:S(2)}) collective-permute-start(bf16[2,16,1024]{2,1,0:T(8,128)(2,1)S(1)} %get-tuple-element.41), channel_id=1, source_target_pairs={{0,9},{1,8},{2,11},{3,10},{4,13},{5,12},{6,15},{7,14},{8,1},{9,0},... | collective-permute-start | bytes 196616 | tf_op jit(solution)/shard_map/ppermute | solution.py:297
  24.5 10.8 %collective-permute-start.11 = (bf16[2,16,1024]{2,1,0:T(8,128)(2,1)S(1)}, bf16[2,16,1024]{2,1,0:T(8,128)(2,1)S(1)}, u32[]{:S(2)}, u32[]{:S(2)}) collective-permute-start(bf16[2,16,1024]{2,1,0:T(8,128)(2,1)S(1)} %get-tuple-element.53), channel_id=1, source_target_pairs={{0,17},{1,16},{2,19},{3,18},{4,21},{5,20},{6,23},{7,22},{8,25},{9,... | collective-permute-start | bytes 196616 | tf_op jit(solution)/shard_map/ppermute | solution.py:297
  25.9 10.0 %collective-permute-start.12 = (bf16[2,16,1024]{2,1,0:T(8,128)(2,1)S(1)}, bf16[2,16,1024]{2,1,0:T(8,128)(2,1)S(1)}, u32[]{:S(2)}, u32[]{:S(2)}) collective-permute-start(bf16[2,16,1024]{2,1,0:T(8,128)(2,1)S(1)} %get-tuple-element.54), channel_id=1, source_target_pairs={{0,9},{1,8},{2,11},{3,10},{4,13},{5,12},{6,15},{7,14},{8,1},{9,0},... | collective-permute-start | bytes 196616 | tf_op jit(solution)/shard_map/ppermute | solution.py:297
  29.7 6.1 %collective-permute-start.13 = (bf16[2,16,1024]{2,1,0:T(8,128)(2,1)S(1)}, bf16[2,16,1024]{2,1,0:T(8,128)(2,1)S(1)}, u32[]{:S(2)}, u32[]{:S(2)}) collective-permute-start(bf16[2,16,1024]{2,1,0:T(8,128)(2,1)S(1)} %get-tuple-element.55), channel_id=1, source_target_pairs={{0,17},{1,16},{2,19},{3,18},{4,21},{5,20},{6,23},{7,22},{8,25},{9,... | collective-permute-start | bytes 196616 | tf_op jit(solution)/shard_map/ppermute | solution.py:297
  31.1 5.3 %collective-permute-start.1 = (bf16[2,16,1024]{2,1,0:T(8,128)(2,1)S(1)}, bf16[2,16,1024]{2,1,0:T(8,128)(2,1)S(1)}, u32[]{:S(2)}, u32[]{:S(2)}) collective-permute-start(bf16[2,16,1024]{2,1,0:T(8,128)(2,1)S(1)} %get-tuple-element.42), channel_id=1, source_target_pairs={{0,17},{1,16},{2,19},{3,18},{4,21},{5,20},{6,23},{7,22},{8,25},{9,... | collective-permute-start | bytes 196616 | tf_op jit(solution)/shard_map/ppermute | solution.py:297
  33.6 1.0 %copy-start.1 = (bf16[1024,256]{1,0:T(8,128)(2,1)S(1)}, bf16[1024,256]{1,0:T(8,128)(2,1)}, u32[]{:S(2)}) copy-start(bf16[1024,256]{1,0:T(8,128)(2,1)} %constant.12.refs_6_.refs_7_.refs_8_.refs_9_) | copy-start | bytes 1572868
  33.6 1.2 %copy-start.2 = (bf16[1024,256]{1,0:T(8,128)(2,1)S(1)}, bf16[1024,256]{1,0:T(8,128)(2,1)}, u32[]{:S(2)}) copy-start(bf16[1024,256]{1,0:T(8,128)(2,1)} %constant.9.refs_5_.refs_6_.refs_7_.refs_8_) | copy-start | bytes 1572868

commit v3 on v2

--- a/solution.py
+++ b/solution.py
@@ -167,9 +167,10 @@
     extra[...] = tails[...]
     group = (out.shape[2] - 8) // rounds
     zones = rows // group
+    first_zone = out.shape[1] - (part + 1) * zones
     for earlier, ref in enumerate(done):
-        out[:, earlier * zones : (earlier + 1) * zones] = ref[:, earlier * zones : (earlier + 1) * zones]
-    first_zone = part * zones
+        start = out.shape[1] - (earlier + 1) * zones
+        out[:, start : start + zones] = ref[:, start : start + zones]
     diagonal = lax.broadcasted_iota(jnp.int32, (rows, LANES), 0) == lax.broadcasted_iota(jnp.int32, (rows, LANES), 1)
     for pair, slots in enumerate(pairs):
         blocks = [slot ^ here for slot in slots]
@@ -177,7 +178,9 @@
         for side in range(2):
             value = main[pair * rows : (pair + 1) * rows, side * LANES : (side + 1) * LANES]
             value = value.astype(jnp.bfloat16).reshape(zones, group, LANES)
-            out[blocks[side], first_zone : first_zone + zones, step * group : (step + 1) * group, :] = value
+            for zone in range(zones):
+                place = first_zone + zones - 1 - zone
+                out[blocks[side], place, step * group : (step + 1) * group, :] = value[zone]
             mirror = main[pair * rows : (pair + 1) * rows, (1 - side) * LANES : (1 - side) * LANES + 1]
             end = jnp.sum(jnp.where(diagonal, mirror, 0.0), axis=0, keepdims=True)
             extra[blocks[side], step : step + 1, :] = end
@@ -347,7 +350,7 @@
             )(*heads, *sent, early, stack, tails, lag_hi, lag_lo)
         )
     sent = sent[-1]
-    same_half = [[a * time_count + z * 2 + c for a in range(chan_count) for z in range(zones)] for c in range(2)]
+    same_half = [[a * time_count + z * 2 + c for a in range(chan_count) for z in reversed(range(zones))] for c in range(2)]
     parts = lax.all_to_all(
         sent.reshape(chan_count * zones, height, LANES),
         ("chan", "tm"),

time: 55.3 us -> 51.7 us (0.935)
  blocking collectives: 17.4 us -> 13.8 us
    all_to_all x1, blocking collectives: 17.4 us -> 13.8 us  [by_channels(): lax.all_to_all(sent.reshape(chan_count * zones, height, LANES), ('chan',...]
  transfers between devices with their start and end apart: 14 -> 14, of which waited for: 4 -> 4; matrix products, arithmetic and copies ran while one was open for 0% -> 0% of each run, Pallas kernels for 9% -> 10%
where the time goes in v3:
time: 51.7 us; the launch traced here: 51.5 us
  blocking collectives  13.8 us (27%)
  starting transfers between devices  13.6 us (26%)
  waiting for transfers between devices  12.6 us (24%)
  Pallas kernels  10.1 us (20%)
  local copies, waits for them, and re-layouts  1.15 us (2%)
    all_to_all x1, blocking collectives, by_channels(): lax.all_to_all(sent.reshape(chan_count * zones, height, LANES), ('chan',...  13.8 us
    ppermute x13, starting transfers between devices, by_channels(): piece = lax.ppermute(piece, ('chan', 'tm'), partners(*key))  13.1 us
    ppermute x13, waiting for transfers between devices, by_channels(): piece = lax.ppermute(piece, ('chan', 'tm'), partners(*key))  12.6 us
    pallas_call x2, Pallas kernels, cut(): pl.pallas_call(functools.partial(cut_kernel, keys, zone_ranges), out_shap...  2.6 us
    pallas_call x1, Pallas kernels, by_channels(): pl.pallas_call(functools.partial(early_kernel, early_slots), out_shape=[j...  2.13 us
    pallas_call x1, Pallas kernels, by_channels(): pl.pallas_call(functools.partial(sent_kernel, len(late_raw)), out_shape=[...  2.08 us
    pallas_call x4, Pallas kernels, by_channels(): pl.pallas_call(functools.partial(second_kernel, rounds, early_slots, late...  2 us
    unnamed x10, local copies, waits for them, and re-layouts  1.15 us
  transfers between devices with their start and end apart: 14, of which 4 were waited for; matrix products, arithmetic and copies ran while one was open for 0% of the time, Pallas kernels for 10%

profile of v3, /device:TPU:0, one launch (start us, length us, event | category | flops | bytes accessed | tf_op | source)
XLA Modules:
  0.0 51.5 jit_solution(17099816136135595284)
XLA Ops:
  0.0 1.6 %shard_map.64 = (bf16[2,4,16,1024]{3,2,1,0:T(8,128)(2,1)S(1)}, bf16[2,4,16,1024]{3,2,1,0:T(8,128)(2,1)S(1)}, bf16[2,4,16,1024]{3,2,1,0:T(8,128)(2,1)S(1)}, bf16[...) custom-call(bf16[2,4,2,4,16,1024]{5,4,3,2,1,0:T(8,128)(2,1)} %bitcast.34), custom_call_target="tpu_custom_call" | custom-call | tf_op jit(solution)/shard_map/pallas_call | solution.py:253
  1.7 0.5 copy-done
  2.2 2.1 %whiten_sent.1 = (bf16[2,64,1024]{2,1,0:T(8,128)(2,1)S(1)}, bf16[2,64,1024]{2,1,0:T(8,128)(2,1)S(1)}, bf16[2,16,1024]{2,1,0:T(8,128)(2,1)S(1)}, bf16[2,16,1024]{...) custom-call(s32[2,4]{1,0:T(2,128)S(1)} %copy-done.3, ...), custom_call_target="tpu_custom_call" | custom-call | tf_op jit(solution)/shard_map/whiten_sent/pallas_call | solution.py:288
  4.2 2.5 %collective-permute-start.2 = (bf16[2,16,1024]{2,1,0:T(8,128)(2,1)S(1)}, bf16[2,16,1024]{2,1,0:T(8,128)(2,1)S(1)}, u32[]{:S(2)}, u32[]{:S(2)}) collective-permute-start(bf16[2,16,1024]{2,1,0:T(8,128)(2,1)S(1)} %get-tuple-element.43), channel_id=1, source_target_pairs={{0,9},{1,8},{2,11},{3,10},{4,13},{5,12},{6,15},{7,14},{8,1},{9,0},... | collective-permute-start | bytes 196616 | tf_op jit(solution)/shard_map/ppermute | solution.py:300
  6.7 1.8 %collective-permute-start.3 = (bf16[2,16,1024]{2,1,0:T(8,128)(2,1)S(1)}, bf16[2,16,1024]{2,1,0:T(8,128)(2,1)S(1)}, u32[]{:S(2)}, u32[]{:S(2)}) collective-permute-start(bf16[2,16,1024]{2,1,0:T(8,128)(2,1)S(1)} %get-tuple-element.44), channel_id=1, source_target_pairs={{0,17},{1,16},{2,19},{3,18},{4,21},{5,20},{6,23},{7,22},{8,25},{9,... | collective-permute-start | bytes 196616 | tf_op jit(solution)/shard_map/ppermute | solution.py:300
  8.5 0.1 collective-permute-start.10
  8.6 0.6 %collective-permute-start.4 = (s32[2,4]{1,0:T(2,128)S(1)}, s32[2,4]{1,0:T(2,128)S(1)}, u32[]{:S(2)}, u32[]{:S(2)}) collective-permute-start(s32[2,4]{1,0:T(2,128)S(1)} %copy-done.3), channel_id=1, source_target_pairs={{0,1},{1,0},{2,3},{3,2},{4,5},{5,4},{6,7},{7,6},{8,9},{9,8},{10,11... | collective-permute-start | bytes 104 | tf_op jit(solution)/shard_map/ppermute | solution.py:306
  9.2 1.0 %shard_map.65 = bf16[2,4,16,1024]{3,2,1,0:T(8,128)(2,1)S(1)} custom-call(bf16[2,4,2,4,16,1024]{5,4,3,2,1,0:T(8,128)(2,1)} %bitcast.35), custom_call_target="tpu_custom_call" | custom-call | tf_op jit(solution)/shard_map/pallas_call | solution.py:253
  10.1 1.5 %collective-permute-start.5 = (bf16[2,64,1024]{2,1,0:T(8,128)(2,1)S(1)}, bf16[2,64,1024]{2,1,0:T(8,128)(2,1)S(1)}, u32[]{:S(2)}, u32[]{:S(2)}) collective-permute-start(bf16[2,64,1024]{2,1,0:T(8,128)(2,1)S(1)} %bitcast.21), channel_id=1, source_target_pairs={{0,24},{1,25},{2,26},{3,27},{4,28},{5,29},{6,30},{7,31},{8,16},{9,... | collective-permute-start | bytes 786440 | tf_op jit(solution)/shard_map/ppermute | solution.py:300
  11.6 0.1 collective-permute-start.8
  11.8 1.9 %collective-permute-start.9 = (bf16[2,64,1024]{2,1,0:T(8,128)(2,1)S(1)}, bf16[2,64,1024]{2,1,0:T(8,128)(2,1)S(1)}, u32[]{:S(2)}, u32[]{:S(2)}) collective-permute-start(bf16[2,64,1024]{2,1,0:T(8,128)(2,1)S(1)} %get-tuple-element.50), channel_id=1, source_target_pairs={{0,16},{1,17},{2,18},{3,19},{4,20},{5,21},{6,22},{7,23},{8,24},{9,... | collective-permute-start | bytes 786440 | tf_op jit(solution)/shard_map/ppermute | solution.py:300
  13.7 0.2 collective-permute-start.6
  13.9 1.3 %collective-permute-start.7 = (bf16[2,64,1024]{2,1,0:T(8,128)(2,1)S(1)}, bf16[2,64,1024]{2,1,0:T(8,128)(2,1)S(1)}, u32[]{:S(2)}, u32[]{:S(2)}) collective-permute-start(bf16[2,64,1024]{2,1,0:T(8,128)(2,1)S(1)} %bitcast.32), channel_id=1, source_target_pairs={{0,1},{1,0},{2,3},{3,2},{4,5},{5,4},{6,7},{7,6},{8,9},{9,8},{10,11... | collective-permute-start | bytes 786440 | tf_op jit(solution)/shard_map/ppermute | solution.py:300
  15.3 5.1 %collective-permute-done.5.refs_0_ = bf16[2,64,1024]{2,1,0:T(8,128)(2,1)S(1)} collective-permute-done((bf16[2,64,1024]{2,1,0:T(8,128)(2,1)S(1)}, bf16[2,64,1024]{2,1,0:T(8,128)(2,1)S(1)}, u32[]{:S(2)}, u32[]{:S(2)}) %collective-permute-start.5) | collective-permute-done | bytes 262176 | tf_op jit(solution)/shard_map/ppermute | solution.py:300
  20.3 4.2 %collective-permute-done.8.refs_0_ = bf16[2,64,1024]{2,1,0:T(8,128)(2,1)S(1)} collective-permute-done((bf16[2,64,1024]{2,1,0:T(8,128)(2,1)S(1)}, bf16[2,64,1024]{2,1,0:T(8,128)(2,1)S(1)}, u32[]{:S(2)}, u32[]{:S(2)}) %collective-permute-start.8) | collective-permute-done | bytes 262176 | tf_op jit(solution)/shard_map/ppermute | solution.py:300
  24.5 1.3 %collective-permute-done.9.refs_1_ = bf16[2,64,1024]{2,1,0:T(8,128)(2,1)S(1)} collective-permute-done((bf16[2,64,1024]{2,1,0:T(8,128)(2,1)S(1)}, bf16[2,64,1024]{2,1,0:T(8,128)(2,1)S(1)}, u32[]{:S(2)}, u32[]{:S(2)}) %collective-permute-start.9) | collective-permute-done | bytes 262176 | tf_op jit(solution)/shard_map/ppermute | solution.py:300
  25.9 1.9 %collective-permute-start.12 = (bf16[2,16,1024]{2,1,0:T(8,128)(2,1)S(1)}, bf16[2,16,1024]{2,1,0:T(8,128)(2,1)S(1)}, u32[]{:S(2)}, u32[]{:S(2)}) collective-permute-start(bf16[2,16,1024]{2,1,0:T(8,128)(2,1)S(1)} %get-tuple-element.54), channel_id=1, source_target_pairs={{0,9},{1,8},{2,11},{3,10},{4,13},{5,12},{6,15},{7,14},{8,1},{9,0},... | collective-permute-start | bytes 196616 | tf_op jit(solution)/shard_map/ppermute | solution.py:300
  27.7 2.0 %collective-permute-done.6.refs_1_ = bf16[2,64,1024]{2,1,0:T(8,128)(2,1)S(1)} collective-permute-done((bf16[2,64,1024]{2,1,0:T(8,128)(2,1)S(1)}, bf16[2,64,1024]{2,1,0:T(8,128)(2,1)S(1)}, u32[]{:S(2)}, u32[]{:S(2)}) %collective-permute-start.6) | collective-permute-done | bytes 262176 | tf_op jit(solution)/shard_map/ppermute | solution.py:300
  29.7 1.3 %collective-permute-start.13 = (bf16[2,16,1024]{2,1,0:T(8,128)(2,1)S(1)}, bf16[2,16,1024]{2,1,0:T(8,128)(2,1)S(1)}, u32[]{:S(2)}, u32[]{:S(2)}) collective-permute-start(bf16[2,16,1024]{2,1,0:T(8,128)(2,1)S(1)} %get-tuple-element.55), channel_id=1, source_target_pairs={{0,17},{1,16},{2,19},{3,18},{4,21},{5,20},{6,23},{7,22},{8,25},{9,... | collective-permute-start | bytes 196616 | tf_op jit(solution)/shard_map/ppermute | solution.py:300
  31.1 0.4 collective-permute-start.1
  31.5 2.1 %early.1 = (bf16[4,2,64,1024]{3,2,1,0:T(8,128)(2,1)S(1)}, f32[4,8,128]{2,1,0:T(8,128)S(1)}, f32[3,8,128]{2,1,0:T(8,128)S(1)}) custom-call(s32[3,4]{1,0:T(4,128)S(1)} %copy-done.4, s32[2,4]{1,0:T(2,128)S(1)} %copy-done.3, s32[2,4]{1,0:T(2,128)S(1)} %collective-permute-done.4.other, bf16[2,64,1024]{2,1,0:T(8,128)(2,1)S(1)} %collective-permute-done.5.refs_0_, ...), custom_call_target="tpu_custom_call" | custom-call | tf_op jit(solution)/shard_map/early/pallas_call | solution.py:312
  33.6 0.0 copy-start.1
  33.6 0.0 copy-start.2
  33.6 0.5 %first_half.1.refs_3_.refs_4_.refs_5_.refs_6_ = f32[6,64,1024]{2,1,0:T(8,128)S(1)} custom-call(bf16[2,64,1024]{2,1,0:T(8,128)(2,1)S(1)} %collective-permute-done.8.refs_0_, bf16[2,64,1024]{2,1,0:T(8,128)(2,1)S(1)} %collective-permute-done.9.refs_1_, bf16[4,2,64,1024]{3,2,1,0:T(8,128)(2,1)S(1)} %get-tuple-element.48.refs_2_.refs_3_.refs_4_.refs_5_), custom_call_target="tpu_custom_call" | custom-call | tf_op jit(solution)/shard_map/first_half/pallas_call | solution.py:325
  34.2 0.5 copy-done.1
  34.7 0.2 copy-done.2
  34.8 0.5 shard_map.66.refs_2_
  35.3 0.5 shard_map.67.refs_3_
  35.9 0.5 shard_map.68.refs_4_
  36.4 0.5 shard_map.69
  36.9 13.8 %all_to_all.5 = bf16[16,56,128]{2,1,0:T(8,128)(2,1)S(1)} all-to-all(bf16[16,56,128]{2,1,0:T(8,128)(2,1)S(1)} %bitcast.19), channel_id=1, replica_groups={{6,4,2,0,14,12,10,8,22,20,18,16,30,28,26,24},{7,5,3,1,15,13,11,9,23,21,..., dimensions={0} | all-to-all | bytes 458752 | tf_op jit(solution)/shard_map/all_to_all | solution.py:354
  50.7 0.8 %finish.1 = f32[3,64,129]{2,1,0:T(8,128)} custom-call(bf16[4,4,56,128]{3,2,1,0:T(8,128)(2,1)S(1)} %bitcast.18, f32[3,8,128]{2,1,0:T(8,128)S(1)} %get-tuple-element.56.order), custom_call_target="tpu_custom_call" | custom-call | tf_op jit(solution)/shard_map/finish/pallas_call | solution.py:362
  (17 shorter events, 0.0 us)
Async XLA Ops:
  0.0 2.1 %copy-start = (bf16[1024,1024]{1,0:T(8,128)(2,1)S(1)}, bf16[1024,1024]{1,0:T(8,128)(2,1)}, u32[]{:S(2)}) copy-start(bf16[1024,1024]{1,0:T(8,128)(2,1)} %constant.8.refs_10_.refs_4_) | copy-start | bytes 6291460
  0.0 2.1 %copy-start.3 = (s32[2,4]{1,0:T(2,128)S(1)}, s32[2,4]{1,0:T(2,128)}, u32[]{:S(2)}) copy-start(s32[2,4]{1,0:T(2,128)} %valid.3) | copy-start | bytes 100
  2.1 29.3 %copy-start.4 = (s32[3,4]{1,0:T(4,128)S(1)}, s32[3,4]{1,0:T(4,128)}, u32[]{:S(2)}) copy-start(s32[3,4]{1,0:T(4,128)} %plan.1) | copy-start | bytes 148
  4.2 7.5 %collective-permute-start.2 = (bf16[2,16,1024]{2,1,0:T(8,128)(2,1)S(1)}, bf16[2,16,1024]{2,1,0:T(8,128)(2,1)S(1)}, u32[]{:S(2)}, u32[]{:S(2)}) collective-permute-start(bf16[2,16,1024]{2,1,0:T(8,128)(2,1)S(1)} %get-tuple-element.43), channel_id=1, source_target_pairs={{0,9},{1,8},{2,11},{3,10},{4,13},{5,12},{6,15},{7,14},{8,1},{9,0},... | collective-permute-start | bytes 196616 | tf_op jit(solution)/shard_map/ppermute | solution.py:300
  6.7 7.0 %collective-permute-start.3 = (bf16[2,16,1024]{2,1,0:T(8,128)(2,1)S(1)}, bf16[2,16,1024]{2,1,0:T(8,128)(2,1)S(1)}, u32[]{:S(2)}, u32[]{:S(2)}) collective-permute-start(bf16[2,16,1024]{2,1,0:T(8,128)(2,1)S(1)} %get-tuple-element.44), channel_id=1, source_target_pairs={{0,17},{1,16},{2,19},{3,18},{4,21},{5,20},{6,23},{7,22},{8,25},{9,... | collective-permute-start | bytes 196616 | tf_op jit(solution)/shard_map/ppermute | solution.py:300
  8.5 5.4 %collective-permute-start.10 = (bf16[2,16,1024]{2,1,0:T(8,128)(2,1)S(1)}, bf16[2,16,1024]{2,1,0:T(8,128)(2,1)S(1)}, u32[]{:S(2)}, u32[]{:S(2)}) collective-permute-start(bf16[2,16,1024]{2,1,0:T(8,128)(2,1)S(1)} %get-tuple-element.52), channel_id=1, source_target_pairs={{0,9},{1,8},{2,11},{3,10},{4,13},{5,12},{6,15},{7,14},{8,1},{9,0},... | collective-permute-start | bytes 196616 | tf_op jit(solution)/shard_map/ppermute | solution.py:300
  8.6 3.0 %collective-permute-start.4 = (s32[2,4]{1,0:T(2,128)S(1)}, s32[2,4]{1,0:T(2,128)S(1)}, u32[]{:S(2)}, u32[]{:S(2)}) collective-permute-start(s32[2,4]{1,0:T(2,128)S(1)} %copy-done.3), channel_id=1, source_target_pairs={{0,1},{1,0},{2,3},{3,2},{4,5},{5,4},{6,7},{7,6},{8,9},{9,8},{10,11... | collective-permute-start | bytes 104 | tf_op jit(solution)/shard_map/ppermute | solution.py:306
  10.1 10.2 %collective-permute-start.5 = (bf16[2,64,1024]{2,1,0:T(8,128)(2,1)S(1)}, bf16[2,64,1024]{2,1,0:T(8,128)(2,1)S(1)}, u32[]{:S(2)}, u32[]{:S(2)}) collective-permute-start(bf16[2,64,1024]{2,1,0:T(8,128)(2,1)S(1)} %bitcast.21), channel_id=1, source_target_pairs={{0,24},{1,25},{2,26},{3,27},{4,28},{5,29},{6,30},{7,31},{8,16},{9,... | collective-permute-start | bytes 786440 | tf_op jit(solution)/shard_map/ppermute | solution.py:300
  11.6 12.9 %collective-permute-start.8 = (bf16[2,64,1024]{2,1,0:T(8,128)(2,1)S(1)}, bf16[2,64,1024]{2,1,0:T(8,128)(2,1)S(1)}, u32[]{:S(2)}, u32[]{:S(2)}) collective-permute-start(bf16[2,64,1024]{2,1,0:T(8,128)(2,1)S(1)} %get-tuple-element.49), channel_id=1, source_target_pairs={{0,8},{1,9},{2,10},{3,11},{4,12},{5,13},{6,14},{7,15},{8,0},{9,1},... | collective-permute-start | bytes 786440 | tf_op jit(solution)/shard_map/ppermute | solution.py:300
  11.8 14.1 %collective-permute-start.9 = (bf16[2,64,1024]{2,1,0:T(8,128)(2,1)S(1)}, bf16[2,64,1024]{2,1,0:T(8,128)(2,1)S(1)}, u32[]{:S(2)}, u32[]{:S(2)}) collective-permute-start(bf16[2,64,1024]{2,1,0:T(8,128)(2,1)S(1)} %get-tuple-element.50), channel_id=1, source_target_pairs={{0,16},{1,17},{2,18},{3,19},{4,20},{5,21},{6,22},{7,23},{8,24},{9,... | collective-permute-start | bytes 786440 | tf_op jit(solution)/shard_map/ppermute | solution.py:300
  13.7 16.0 %collective-permute-start.6 = (bf16[2,64,1024]{2,1,0:T(8,128)(2,1)S(1)}, bf16[2,64,1024]{2,1,0:T(8,128)(2,1)S(1)}, u32[]{:S(2)}, u32[]{:S(2)}) collective-permute-start(bf16[2,64,1024]{2,1,0:T(8,128)(2,1)S(1)} %bitcast.33), channel_id=1, source_target_pairs={{0,25},{1,24},{2,27},{3,26},{4,29},{5,28},{6,31},{7,30},{8,17},{9,... | collective-permute-start | bytes 786440 | tf_op jit(solution)/shard_map/ppermute | solution.py:300
  13.9 17.2 %collective-permute-start.7 = (bf16[2,64,1024]{2,1,0:T(8,128)(2,1)S(1)}, bf16[2,64,1024]{2,1,0:T(8,128)(2,1)S(1)}, u32[]{:S(2)}, u32[]{:S(2)}) collective-permute-start(bf16[2,64,1024]{2,1,0:T(8,128)(2,1)S(1)} %bitcast.32), channel_id=1, source_target_pairs={{0,1},{1,0},{2,3},{3,2},{4,5},{5,4},{6,7},{7,6},{8,9},{9,8},{10,11... | collective-permute-start | bytes 786440 | tf_op jit(solution)/shard_map/ppermute | solution.py:300
  20.3 16.0 %collective-permute-start = (bf16[2,16,1024]{2,1,0:T(8,128)(2,1)S(1)}, bf16[2,16,1024]{2,1,0:T(8,128)(2,1)S(1)}, u32[]{:S(2)}, u32[]{:S(2)}) collective-permute-start(bf16[2,16,1024]{2,1,0:T(8,128)(2,1)S(1)} %get-tuple-element.41), channel_id=1, source_target_pairs={{0,9},{1,8},{2,11},{3,10},{4,13},{5,12},{6,15},{7,14},{8,1},{9,0},... | collective-permute-start | bytes 196616 | tf_op jit(solution)/shard_map/ppermute | solution.py:300
  24.5 10.8 %collective-permute-start.11 = (bf16[2,16,1024]{2,1,0:T(8,128)(2,1)S(1)}, bf16[2,16,1024]{2,1,0:T(8,128)(2,1)S(1)}, u32[]{:S(2)}, u32[]{:S(2)}) collective-permute-start(bf16[2,16,1024]{2,1,0:T(8,128)(2,1)S(1)} %get-tuple-element.53), channel_id=1, source_target_pairs={{0,17},{1,16},{2,19},{3,18},{4,21},{5,20},{6,23},{7,22},{8,25},{9,... | collective-permute-start | bytes 196616 | tf_op jit(solution)/shard_map/ppermute | solution.py:300
  25.9 10.0 %collective-permute-start.12 = (bf16[2,16,1024]{2,1,0:T(8,128)(2,1)S(1)}, bf16[2,16,1024]{2,1,0:T(8,128)(2,1)S(1)}, u32[]{:S(2)}, u32[]{:S(2)}) collective-permute-start(bf16[2,16,1024]{2,1,0:T(8,128)(2,1)S(1)} %get-tuple-element.54), channel_id=1, source_target_pairs={{0,9},{1,8},{2,11},{3,10},{4,13},{5,12},{6,15},{7,14},{8,1},{9,0},... | collective-permute-start | bytes 196616 | tf_op jit(solution)/shard_map/ppermute | solution.py:300
  29.7 6.1 %collective-permute-start.13 = (bf16[2,16,1024]{2,1,0:T(8,128)(2,1)S(1)}, bf16[2,16,1024]{2,1,0:T(8,128)(2,1)S(1)}, u32[]{:S(2)}, u32[]{:S(2)}) collective-permute-start(bf16[2,16,1024]{2,1,0:T(8,128)(2,1)S(1)} %get-tuple-element.55), channel_id=1, source_target_pairs={{0,17},{1,16},{2,19},{3,18},{4,21},{5,20},{6,23},{7,22},{8,25},{9,... | collective-permute-start | bytes 196616 | tf_op jit(solution)/shard_map/ppermute | solution.py:300
  31.1 5.3 %collective-permute-start.1 = (bf16[2,16,1024]{2,1,0:T(8,128)(2,1)S(1)}, bf16[2,16,1024]{2,1,0:T(8,128)(2,1)S(1)}, u32[]{:S(2)}, u32[]{:S(2)}) collective-permute-start(bf16[2,16,1024]{2,1,0:T(8,128)(2,1)S(1)} %get-tuple-element.42), channel_id=1, source_target_pairs={{0,17},{1,16},{2,19},{3,18},{4,21},{5,20},{6,23},{7,22},{8,25},{9,... | collective-permute-start | bytes 196616 | tf_op jit(solution)/shard_map/ppermute | solution.py:300
  33.6 1.0 %copy-start.1 = (bf16[1024,256]{1,0:T(8,128)(2,1)S(1)}, bf16[1024,256]{1,0:T(8,128)(2,1)}, u32[]{:S(2)}) copy-start(bf16[1024,256]{1,0:T(8,128)(2,1)} %constant.12.refs_6_.refs_7_.refs_8_.refs_9_) | copy-start | bytes 1572868
  33.6 1.2 %copy-start.2 = (bf16[1024,256]{1,0:T(8,128)(2,1)S(1)}, bf16[1024,256]{1,0:T(8,128)(2,1)}, u32[]{:S(2)}) copy-start(bf16[1024,256]{1,0:T(8,128)(2,1)} %constant.9.refs_5_.refs_6_.refs_7_.refs_8_) | copy-start | bytes 1572868
